TPU v7x, 256 devices: a whole 4x4x8 slice. The times are simulated.
256 devices in a mesh: tm: 8 (over x, core), space: 32 (over z, y).
Axes of the slice: x: 4, y: 4, z: 8, core: 2. Of those that a mesh axis runs over, the one named last changes fastest.
Arguments:
- guesses: float32 [8, 512, 4096], P('tm', 'space'), may hold values from -6 to 6
- cond_x: float32 [512, 4096], P('space'), may hold values from 0.025 to 0.24
- cond_y: float32 [512, 4096], P('space'), may hold values from 0.005 to 0.05
- source: float32 [512, 4096], P('space'), may hold values from -0.6 to 0.6
- inflow: float32 [256, 2048], P('space'), may hold values from -6 to 6
Outputs:
- corrected: float32 [8, 512, 4096], P('tm', 'space')
All inputs are finite; a program needn't handle non-finite values.
Results may differ from a plain program's by a relative error of at most 0.00002.
Values sent between devices are 32-bit elements; how exact they have to be, the bound alone decides.
A program may use at most 128 MiB of HBM per device.

v0:
```python
import jax
import jax.numpy as jnp
from jax import lax
from jax.sharding import PartitionSpec as P


def padded(value, sides, width):
    for axis, dim in sides:
        devices, length = (lax.axis_size(axis), value.shape[dim])
        up = [(i, (i + 1) % devices) for i in range(devices - 1)]
        down = [(j, i) for i, j in up]
        last = lax.slice_in_dim(value, length - width, length, axis=dim)
        leading = lax.slice_in_dim(value, 0, width, axis=dim)
        before = lax.ppermute(last, axis, up)
        after = lax.ppermute(leading, axis, down)
        value = jnp.concatenate([before, value, after], axis=dim)
    return value


def from_behind(value, axis, steps):
    count = lax.axis_size(axis)
    leading, last = (max(0, -steps), min(count, count - steps))
    return lax.ppermute(value, axis, [(source, source + steps) for source in range(leading, last)])


def interior(field_ext, cond_rows, cond_cols):
    centre = field_ext[1:-1]
    flux_sum = cond_rows[1:-1] * (field_ext[2:] - centre) - cond_rows[:-2] * (
        centre - field_ext[:-2]
    )
    widened = jnp.pad(centre, ((0, 0), (1, 1)))
    cond_own = cond_cols[1:-1]
    cond_west = jnp.pad(cond_own, ((0, 0), (1, 0)))[:, :-1]
    flux_sum = (
        flux_sum + cond_own * (widened[:, 2:] - centre) - cond_west * (centre - widened[:, :-2])
    )
    return centre + flux_sum


def propagate(field, coef_pad):
    strip_rows = field.shape[0]
    cond_rows = coef_pad[0, 3 : strip_rows + 5]
    cond_cols = coef_pad[1, 3 : strip_rows + 5]
    source_rows = coef_pad[2, 4 : strip_rows + 4]
    for section in range(4):
        extended = padded(field, (("space", 0),), 1)
        field = interior(extended, cond_rows, cond_cols) + source_rows
    return field


def restrict(field):
    lead = field.shape[:-2]
    shaped = field.reshape(lead + (field.shape[-2] // 2, 2, field.shape[-1] // 2, 2))
    return jnp.mean(shaped, axis=(-3, -1))


def shards(guesses, cond_x, cond_y, source, inflow):
    strip_rows = cond_x.shape[0]
    columns = cond_x.shape[1]
    stacked = jnp.stack([cond_x, cond_y, source])
    edge_rows = from_behind(cond_x[strip_rows - 2 :], "space", 1)
    cond_upper = jnp.concatenate([jnp.zeros((2, columns), jnp.float32), edge_rows], axis=0)
    blank_rows = jnp.zeros((4, columns), jnp.float32)
    upper = jnp.stack([cond_upper, blank_rows, blank_rows])
    lower = jnp.zeros((3, 4, columns), jnp.float32)
    coef_pad = jnp.concatenate([upper, stacked, lower], axis=1)
    first_group = lax.axis_index("tm") == 0
    c_point = guesses[0]
    first_pass = propagate(c_point, coef_pad)
    received = from_behind(first_pass, "tm", 1)
    relaxed = jnp.where(first_group, c_point, received)
    second_pass = propagate(relaxed, coef_pad)
    fine_next = from_behind(second_pass, "tm", 1)
    residual = restrict(fine_next - relaxed)
    residual = jnp.where(first_group, 0.0, residual)
    coarse_coef = restrict(coef_pad[:2, 2 : strip_rows + 6])

    def chain_round(index, error_field):
        extended = padded(error_field, (("space", 0),), 1)
        stepped = interior(extended, coarse_coef[0], coarse_coef[1])
        arrived = from_behind(stepped, "tm", 1)
        return jnp.where(first_group, inflow, arrived + residual)

    start_error = jnp.where(first_group, inflow, jnp.zeros_like(residual))
    error_field = lax.fori_loop(0, lax.axis_size("tm") - 1, chain_round, start_error)
    widened = jnp.repeat(jnp.repeat(error_field, 2, axis=0), 2, axis=1)
    return (relaxed + widened)[None]


def solution(mesh):
    return jax.shard_map(
        shards,
        mesh=mesh,
        in_specs=(
            P("tm", "space", None),
            P("space", None),
            P("space", None),
            P("space", None),
            P("space", None),
        ),
        out_specs=P("tm", "space", None),
        check_vma=False,
    )
```

profile of v0, /device:TPU:122, one launch (start us, length us, event | category | flops | bytes accessed | tf_op | source)
XLA Modules:
  0.0 335.4 jit_solution(15772774753161599196)
XLA Ops:
  0.9 4.7 %collective-permute-start.4 = (f32[2,4096]{1,0:T(2,128)S(1)}, f32[2,4096]{1,0:T(2,128)S(1)}, u32[]{:S(2)}, u32[]{:S(2)}) collective-permute-start(f32[2,4096]{1,0:T(2,128)S(1)} %slice.302), channel_id=1, source_target_pairs={{0,1},{1,2},{2,3},{3,4},{4,5},{5,6},{6,7},{7,8},{8,9},{9,10},{10,1... | collective-permute-start | bytes 98312 | tf_op jit(solution)/shard_map/ppermute | solution.py:23
  8.6 7.2 %collective-permute-start.5 = (f32[1,4096]{1,0:T(1,128)S(1)}, f32[1,4096]{1,0:T(1,128)S(1)}, u32[]{:S(2)}, u32[]{:S(2)}) collective-permute-start(f32[1,4096]{1,0:T(1,128)S(1)} %get-tuple-element.126), channel_id=1, source_target_pairs={{0,1},{1,2},{2,3},{3,4},{4,5},{5,6},{6,7},{7,8},{8,9},{9,10},{10,1... | collective-permute-start | bytes 49160 | tf_op jit(solution)/shard_map/ppermute | solution.py:14
  21.5 7.5 %collective-permute-start.7 = (f32[1,4096]{1,0:T(1,128)S(1)}, f32[1,4096]{1,0:T(1,128)S(1)}, u32[]{:S(2)}, u32[]{:S(2)}) collective-permute-start(f32[1,4096]{1,0:T(1,128)S(1)} %get-tuple-element.124), channel_id=1, source_target_pairs={{0,1},{1,2},{2,3},{3,4},{4,5},{5,6},{6,7},{7,8},{8,9},{9,10},{10,1... | collective-permute-start | bytes 49160 | tf_op jit(solution)/shard_map/ppermute | solution.py:14
  34.0 7.5 %collective-permute-start.9 = (f32[1,4096]{1,0:T(1,128)S(1)}, f32[1,4096]{1,0:T(1,128)S(1)}, u32[]{:S(2)}, u32[]{:S(2)}) collective-permute-start(f32[1,4096]{1,0:T(1,128)S(1)} %get-tuple-element.122), channel_id=1, source_target_pairs={{0,1},{1,2},{2,3},{3,4},{4,5},{5,6},{6,7},{7,8},{8,9},{9,10},{10,1... | collective-permute-start | bytes 49160 | tf_op jit(solution)/shard_map/ppermute | solution.py:14
  46.4 7.5 %collective-permute-start.11 = (f32[1,4096]{1,0:T(1,128)S(1)}, f32[1,4096]{1,0:T(1,128)S(1)}, u32[]{:S(2)}, u32[]{:S(2)}) collective-permute-start(f32[1,4096]{1,0:T(1,128)S(1)} %get-tuple-element.120), channel_id=1, source_target_pairs={{0,1},{1,2},{2,3},{3,4},{4,5},{5,6},{6,7},{7,8},{8,9},{9,10},{10,1... | collective-permute-start | bytes 49160 | tf_op jit(solution)/shard_map/ppermute | solution.py:14
  58.8 5.8 %collective-permute-done.12 = f32[16,4096]{1,0:T(8,128)S(1)} collective-permute-done((f32[16,4096]{1,0:T(8,128)S(1)}, f32[16,4096]{1,0:T(8,128)S(1)}, u32[]{:S(2)}, u32[]{:S(2)}) %collective-permute-start.12) | collective-permute-done | bytes 262176 | tf_op jit(solution)/shard_map/ppermute | solution.py:23
  67.5 7.5 %collective-permute-start.14 = (f32[1,4096]{1,0:T(1,128)S(1)}, f32[1,4096]{1,0:T(1,128)S(1)}, u32[]{:S(2)}, u32[]{:S(2)}) collective-permute-start(f32[1,4096]{1,0:T(1,128)S(1)} %get-tuple-element.118), channel_id=1, source_target_pairs={{0,1},{1,2},{2,3},{3,4},{4,5},{5,6},{6,7},{7,8},{8,9},{9,10},{10,1... | collective-permute-start | bytes 49160 | tf_op jit(solution)/shard_map/ppermute | solution.py:14
  80.0 7.5 %collective-permute-start.16 = (f32[1,4096]{1,0:T(1,128)S(1)}, f32[1,4096]{1,0:T(1,128)S(1)}, u32[]{:S(2)}, u32[]{:S(2)}) collective-permute-start(f32[1,4096]{1,0:T(1,128)S(1)} %get-tuple-element.116), channel_id=1, source_target_pairs={{0,1},{1,2},{2,3},{3,4},{4,5},{5,6},{6,7},{7,8},{8,9},{9,10},{10,1... | collective-permute-start | bytes 49160 | tf_op jit(solution)/shard_map/ppermute | solution.py:14
  92.4 7.5 %collective-permute-start.18 = (f32[1,4096]{1,0:T(1,128)S(1)}, f32[1,4096]{1,0:T(1,128)S(1)}, u32[]{:S(2)}, u32[]{:S(2)}) collective-permute-start(f32[1,4096]{1,0:T(1,128)S(1)} %get-tuple-element.114), channel_id=1, source_target_pairs={{0,1},{1,2},{2,3},{3,4},{4,5},{5,6},{6,7},{7,8},{8,9},{9,10},{10,1... | collective-permute-start | bytes 49160 | tf_op jit(solution)/shard_map/ppermute | solution.py:14
  104.9 7.5 %collective-permute-start.20 = (f32[1,4096]{1,0:T(1,128)S(1)}, f32[1,4096]{1,0:T(1,128)S(1)}, u32[]{:S(2)}, u32[]{:S(2)}) collective-permute-start(f32[1,4096]{1,0:T(1,128)S(1)} %get-tuple-element.112), channel_id=1, source_target_pairs={{0,1},{1,2},{2,3},{3,4},{4,5},{5,6},{6,7},{7,8},{8,9},{9,10},{10,1... | collective-permute-start | bytes 49160 | tf_op jit(solution)/shard_map/ppermute | solution.py:14
  114.1 44.6 %reshape.31 = f32[2,10,2,2048,2]{4,3,0,2,1:T(8,128)} reshape(f32[2,20,4096]{2,0,1:T(2,128)S(1)} %copy.158) | data formatting | bytes 1310720 | tf_op jit(solution)/shard_map/reshape | solution.py:53
  158.6 16.4 %reduce_sum.18 = f32[2,10,2048]{2,0,1:T(2,128)S(1)} reduce(f32[2,10,2,2048,2]{4,3,0,2,1:T(8,128)} %reshape.31, f32[]{:T(128)} %constant.33.clone.1), dimensions={2,4}, to_apply=%region_0.1 | reduce | flops 122880 | bytes 819204 | tf_op jit(solution)/shard_map/reduce_sum | solution.py:54
  177.7 5.4 %collective-permute-done.21 = f32[16,4096]{1,0:T(8,128)S(1)} collective-permute-done((f32[16,4096]{1,0:T(8,128)S(1)}, f32[16,4096]{1,0:T(8,128)S(1)}, u32[]{:S(2)}, u32[]{:S(2)}) %collective-permute-start.21) | collective-permute-done | bytes 262176 | tf_op jit(solution)/shard_map/ppermute | solution.py:23
  183.2 23.7 %reshape.32 = f32[8,2,2048,2]{3,2,1,0:T(8,128)} reshape(f32[16,4096]{1,0:T(8,128)S(1)} %sub.231) | data formatting | bytes 524288 | tf_op jit(solution)/shard_map/reshape | solution.py:53
  206.9 8.0 %reduce_sum.19 = f32[8,2048]{1,0:T(8,128)S(1)} reduce(f32[8,2,2048,2]{3,2,1,0:T(8,128)} %reshape.32, f32[]{:T(128)} %constant.33.clone.1), dimensions={1,3}, to_apply=%region_1.2 | reduce | flops 49152 | bytes 327684 | tf_op jit(solution)/shard_map/reduce_sum | solution.py:54
  214.9 117.9 %while.12 = (s32[]{:T(128)}, f32[8,2048]{1,0:T(8,128)S(1)}, pred[]{:T(512)}, f32[2,10,2048]{2,1,0:T(8,128)S(1)}, f32[8,2048]{1,0:T(8,128)S(1)}, /*index=5*/f32[8,2048]{1,0:T(8,128)S(1)}, s32[]{:T(128)}) while((s32[]{:T(128)}, f32[8,2048]{1,0:T(8,128)S(1)}, pred[]{:T(512)}, f32[2,10,2048]{2,1,0:T(8,128)S(1)}, f32[8,2048]{1,0:T(8,128)S(1)}, ...), condition=%wide.region_3.4_spmd, body=%wide.region_2.3_spmd.sunk | while | flops 262146 | bytes 1097926 | solution.py:85
  214.9 3.9 %collective-permute-start = (f32[1,2048]{1,0:T(1,128)S(1)}, f32[1,2048]{1,0:T(1,128)S(1)}, u32[]{:S(2)}, u32[]{:S(2)}) collective-permute-start(f32[1,2048]{1,0:T(1,128)S(1)} %get-tuple-element.168), channel_id=1, source_target_pairs={{0,1},{1,2},{2,3},{3,4},{4,5},{5,6},{6,7},{7,8},{8,9},{9,10},{10,1... | collective-permute-start | bytes 24584 | tf_op jit(solution)/shard_map/while/body/eval_jaxpr/ppermute | solution.py:14
  220.8 6.9 %collective-permute-done.1 = f32[1,2048]{1,0:T(1,128)S(1)} collective-permute-done((f32[1,2048]{1,0:T(1,128)S(1)}, f32[1,2048]{1,0:T(1,128)S(1)}, u32[]{:S(2)}, u32[]{:S(2)}) %collective-permute-start.1) | collective-permute-done | bytes 8224 | tf_op jit(solution)/shard_map/while/body/eval_jaxpr/ppermute | solution.py:15
  229.8 3.7 %collective-permute-done.2 = f32[8,2048]{1,0:T(8,128)S(1)} collective-permute-done((f32[8,2048]{1,0:T(8,128)S(1)}, f32[8,2048]{1,0:T(8,128)S(1)}, u32[]{:S(2)}, u32[]{:S(2)}) %collective-permute-start.2) | collective-permute-done | bytes 65568 | tf_op jit(solution)/shard_map/while/body/eval_jaxpr/ppermute | solution.py:23
  235.4 3.9 %collective-permute-start.1 = (f32[1,2048]{1,0:T(1,128)S(1)}, f32[1,2048]{1,0:T(1,128)S(1)}, u32[]{:S(2)}, u32[]{:S(2)}) collective-permute-start(f32[1,2048]{1,0:T(1,128)S(1)} %get-tuple-element.169), channel_id=1, source_target_pairs={{1,0},{2,1},{3,2},{4,3},{5,4},{6,5},{7,6},{8,7},{9,8},{10,9},{11,1... | collective-permute-start | bytes 24584 | tf_op jit(solution)/shard_map/while/body/eval_jaxpr/ppermute | solution.py:15
  239.4 4.9 %collective-permute-done.1 = f32[1,2048]{1,0:T(1,128)S(1)} collective-permute-done((f32[1,2048]{1,0:T(1,128)S(1)}, f32[1,2048]{1,0:T(1,128)S(1)}, u32[]{:S(2)}, u32[]{:S(2)}) %collective-permute-start.1) | collective-permute-done | bytes 8224 | tf_op jit(solution)/shard_map/while/body/eval_jaxpr/ppermute | solution.py:15
  246.3 3.7 %collective-permute-done.2 = f32[8,2048]{1,0:T(8,128)S(1)} collective-permute-done((f32[8,2048]{1,0:T(8,128)S(1)}, f32[8,2048]{1,0:T(8,128)S(1)}, u32[]{:S(2)}, u32[]{:S(2)}) %collective-permute-start.2) | collective-permute-done | bytes 65568 | tf_op jit(solution)/shard_map/while/body/eval_jaxpr/ppermute | solution.py:23
  252.0 3.9 %collective-permute-start.1 = (f32[1,2048]{1,0:T(1,128)S(1)}, f32[1,2048]{1,0:T(1,128)S(1)}, u32[]{:S(2)}, u32[]{:S(2)}) collective-permute-start(f32[1,2048]{1,0:T(1,128)S(1)} %get-tuple-element.169), channel_id=1, source_target_pairs={{1,0},{2,1},{3,2},{4,3},{5,4},{6,5},{7,6},{8,7},{9,8},{10,9},{11,1... | collective-permute-start | bytes 24584 | tf_op jit(solution)/shard_map/while/body/eval_jaxpr/ppermute | solution.py:15
  255.9 4.9 %collective-permute-done.1 = f32[1,2048]{1,0:T(1,128)S(1)} collective-permute-done((f32[1,2048]{1,0:T(1,128)S(1)}, f32[1,2048]{1,0:T(1,128)S(1)}, u32[]{:S(2)}, u32[]{:S(2)}) %collective-permute-start.1) | collective-permute-done | bytes 8224 | tf_op jit(solution)/shard_map/while/body/eval_jaxpr/ppermute | solution.py:15
  268.5 3.9 %collective-permute-start.1 = (f32[1,2048]{1,0:T(1,128)S(1)}, f32[1,2048]{1,0:T(1,128)S(1)}, u32[]{:S(2)}, u32[]{:S(2)}) collective-permute-start(f32[1,2048]{1,0:T(1,128)S(1)} %get-tuple-element.169), channel_id=1, source_target_pairs={{1,0},{2,1},{3,2},{4,3},{5,4},{6,5},{7,6},{8,7},{9,8},{10,9},{11,1... | collective-permute-start | bytes 24584 | tf_op jit(solution)/shard_map/while/body/eval_jaxpr/ppermute | solution.py:15
  272.5 4.9 %collective-permute-done.1 = f32[1,2048]{1,0:T(1,128)S(1)} collective-permute-done((f32[1,2048]{1,0:T(1,128)S(1)}, f32[1,2048]{1,0:T(1,128)S(1)}, u32[]{:S(2)}, u32[]{:S(2)}) %collective-permute-start.1) | collective-permute-done | bytes 8224 | tf_op jit(solution)/shard_map/while/body/eval_jaxpr/ppermute | solution.py:15
  285.1 3.9 %collective-permute-start.1 = (f32[1,2048]{1,0:T(1,128)S(1)}, f32[1,2048]{1,0:T(1,128)S(1)}, u32[]{:S(2)}, u32[]{:S(2)}) collective-permute-start(f32[1,2048]{1,0:T(1,128)S(1)} %get-tuple-element.169), channel_id=1, source_target_pairs={{1,0},{2,1},{3,2},{4,3},{5,4},{6,5},{7,6},{8,7},{9,8},{10,9},{11,1... | collective-permute-start | bytes 24584 | tf_op jit(solution)/shard_map/while/body/eval_jaxpr/ppermute | solution.py:15
  289.0 4.9 %collective-permute-done.1 = f32[1,2048]{1,0:T(1,128)S(1)} collective-permute-done((f32[1,2048]{1,0:T(1,128)S(1)}, f32[1,2048]{1,0:T(1,128)S(1)}, u32[]{:S(2)}, u32[]{:S(2)}) %collective-permute-start.1) | collective-permute-done | bytes 8224 | tf_op jit(solution)/shard_map/while/body/eval_jaxpr/ppermute | solution.py:15
  301.6 3.9 %collective-permute-start.1 = (f32[1,2048]{1,0:T(1,128)S(1)}, f32[1,2048]{1,0:T(1,128)S(1)}, u32[]{:S(2)}, u32[]{:S(2)}) collective-permute-start(f32[1,2048]{1,0:T(1,128)S(1)} %get-tuple-element.169), channel_id=1, source_target_pairs={{1,0},{2,1},{3,2},{4,3},{5,4},{6,5},{7,6},{8,7},{9,8},{10,9},{11,1... | collective-permute-start | bytes 24584 | tf_op jit(solution)/shard_map/while/body/eval_jaxpr/ppermute | solution.py:15
  305.6 4.9 %collective-permute-done.1 = f32[1,2048]{1,0:T(1,128)S(1)} collective-permute-done((f32[1,2048]{1,0:T(1,128)S(1)}, f32[1,2048]{1,0:T(1,128)S(1)}, u32[]{:S(2)}, u32[]{:S(2)}) %collective-permute-start.1) | collective-permute-done | bytes 8224 | tf_op jit(solution)/shard_map/while/body/eval_jaxpr/ppermute | solution.py:15
  318.2 3.9 %collective-permute-start.1 = (f32[1,2048]{1,0:T(1,128)S(1)}, f32[1,2048]{1,0:T(1,128)S(1)}, u32[]{:S(2)}, u32[]{:S(2)}) collective-permute-start(f32[1,2048]{1,0:T(1,128)S(1)} %get-tuple-element.169), channel_id=1, source_target_pairs={{1,0},{2,1},{3,2},{4,3},{5,4},{6,5},{7,6},{8,7},{9,8},{10,9},{11,1... | collective-permute-start | bytes 24584 | tf_op jit(solution)/shard_map/while/body/eval_jaxpr/ppermute | solution.py:15
  322.1 4.9 %collective-permute-done.1 = f32[1,2048]{1,0:T(1,128)S(1)} collective-permute-done((f32[1,2048]{1,0:T(1,128)S(1)}, f32[1,2048]{1,0:T(1,128)S(1)}, u32[]{:S(2)}, u32[]{:S(2)}) %collective-permute-start.1) | collective-permute-done | bytes 8224 | tf_op jit(solution)/shard_map/while/body/eval_jaxpr/ppermute | solution.py:15
  (123 shorter events, 94.8 us)
Async XLA Ops:
  0.9 14.9 %collective-permute-start.4 = (f32[2,4096]{1,0:T(2,128)S(1)}, f32[2,4096]{1,0:T(2,128)S(1)}, u32[]{:S(2)}, u32[]{:S(2)}) collective-permute-start(f32[2,4096]{1,0:T(2,128)S(1)} %slice.302), channel_id=1, source_target_pairs={{0,1},{1,2},{2,3},{3,4},{4,5},{5,6},{6,7},{7,8},{8,9},{9,10},{10,1... | collective-permute-start | bytes 98312 | tf_op jit(solution)/shard_map/ppermute | solution.py:23
  6.6 9.3 %collective-permute-start.3 = (f32[1,4096]{1,0:T(1,128)S(1)}, f32[1,4096]{1,0:T(1,128)S(1)}, u32[]{:S(2)}, u32[]{:S(2)}) collective-permute-start(f32[1,4096]{1,0:T(1,128)S(1)} %get-tuple-element.125), channel_id=1, source_target_pairs={{1,0},{2,1},{3,2},{4,3},{5,4},{6,5},{7,6},{8,7},{9,8},{10,9},{11,1... | collective-permute-start | bytes 49160 | tf_op jit(solution)/shard_map/ppermute | solution.py:15
  8.6 8.7 %collective-permute-start.5 = (f32[1,4096]{1,0:T(1,128)S(1)}, f32[1,4096]{1,0:T(1,128)S(1)}, u32[]{:S(2)}, u32[]{:S(2)}) collective-permute-start(f32[1,4096]{1,0:T(1,128)S(1)} %get-tuple-element.126), channel_id=1, source_target_pairs={{0,1},{1,2},{2,3},{3,4},{4,5},{5,6},{6,7},{7,8},{8,9},{9,10},{10,1... | collective-permute-start | bytes 49160 | tf_op jit(solution)/shard_map/ppermute | solution.py:14
  19.6 9.5 %collective-permute-start.6 = (f32[1,4096]{1,0:T(1,128)S(1)}, f32[1,4096]{1,0:T(1,128)S(1)}, u32[]{:S(2)}, u32[]{:S(2)}) collective-permute-start(f32[1,4096]{1,0:T(1,128)S(1)} %get-tuple-element.123), channel_id=1, source_target_pairs={{1,0},{2,1},{3,2},{4,3},{5,4},{6,5},{7,6},{8,7},{9,8},{10,9},{11,1... | collective-permute-start | bytes 49160 | tf_op jit(solution)/shard_map/ppermute | solution.py:15
  21.5 9.0 %collective-permute-start.7 = (f32[1,4096]{1,0:T(1,128)S(1)}, f32[1,4096]{1,0:T(1,128)S(1)}, u32[]{:S(2)}, u32[]{:S(2)}) collective-permute-start(f32[1,4096]{1,0:T(1,128)S(1)} %get-tuple-element.124), channel_id=1, source_target_pairs={{0,1},{1,2},{2,3},{3,4},{4,5},{5,6},{6,7},{7,8},{8,9},{9,10},{10,1... | collective-permute-start | bytes 49160 | tf_op jit(solution)/shard_map/ppermute | solution.py:14
  32.1 9.5 %collective-permute-start.8 = (f32[1,4096]{1,0:T(1,128)S(1)}, f32[1,4096]{1,0:T(1,128)S(1)}, u32[]{:S(2)}, u32[]{:S(2)}) collective-permute-start(f32[1,4096]{1,0:T(1,128)S(1)} %get-tuple-element.121), channel_id=1, source_target_pairs={{1,0},{2,1},{3,2},{4,3},{5,4},{6,5},{7,6},{8,7},{9,8},{10,9},{11,1... | collective-permute-start | bytes 49160 | tf_op jit(solution)/shard_map/ppermute | solution.py:15
  34.0 9.0 %collective-permute-start.9 = (f32[1,4096]{1,0:T(1,128)S(1)}, f32[1,4096]{1,0:T(1,128)S(1)}, u32[]{:S(2)}, u32[]{:S(2)}) collective-permute-start(f32[1,4096]{1,0:T(1,128)S(1)} %get-tuple-element.122), channel_id=1, source_target_pairs={{0,1},{1,2},{2,3},{3,4},{4,5},{5,6},{6,7},{7,8},{8,9},{9,10},{10,1... | collective-permute-start | bytes 49160 | tf_op jit(solution)/shard_map/ppermute | solution.py:14
  44.5 9.5 %collective-permute-start.10 = (f32[1,4096]{1,0:T(1,128)S(1)}, f32[1,4096]{1,0:T(1,128)S(1)}, u32[]{:S(2)}, u32[]{:S(2)}) collective-permute-start(f32[1,4096]{1,0:T(1,128)S(1)} %get-tuple-element.119), channel_id=1, source_target_pairs={{1,0},{2,1},{3,2},{4,3},{5,4},{6,5},{7,6},{8,7},{9,8},{10,9},{11,1... | collective-permute-start | bytes 49160 | tf_op jit(solution)/shard_map/ppermute | solution.py:15
  46.4 9.0 %collective-permute-start.11 = (f32[1,4096]{1,0:T(1,128)S(1)}, f32[1,4096]{1,0:T(1,128)S(1)}, u32[]{:S(2)}, u32[]{:S(2)}) collective-permute-start(f32[1,4096]{1,0:T(1,128)S(1)} %get-tuple-element.120), channel_id=1, source_target_pairs={{0,1},{1,2},{2,3},{3,4},{4,5},{5,6},{6,7},{7,8},{8,9},{9,10},{10,1... | collective-permute-start | bytes 49160 | tf_op jit(solution)/shard_map/ppermute | solution.py:14
  56.9 7.7 %collective-permute-start.12 = (f32[16,4096]{1,0:T(8,128)S(1)}, f32[16,4096]{1,0:T(8,128)S(1)}, u32[]{:S(2)}, u32[]{:S(2)}) collective-permute-start(f32[16,4096]{1,0:T(8,128)S(1)} %fusion.55), channel_id=1, source_target_pairs={{0,32},{32,64},{64,96},{96,128},{128,160},{160,192},{192,224},{1,3... | collective-permute-start | bytes 786440 | tf_op jit(solution)/shard_map/ppermute | solution.py:23
  65.6 9.5 %collective-permute-start.13 = (f32[1,4096]{1,0:T(1,128)S(1)}, f32[1,4096]{1,0:T(1,128)S(1)}, u32[]{:S(2)}, u32[]{:S(2)}) collective-permute-start(f32[1,4096]{1,0:T(1,128)S(1)} %get-tuple-element.117), channel_id=1, source_target_pairs={{1,0},{2,1},{3,2},{4,3},{5,4},{6,5},{7,6},{8,7},{9,8},{10,9},{11,1... | collective-permute-start | bytes 49160 | tf_op jit(solution)/shard_map/ppermute | solution.py:15
  67.5 9.0 %collective-permute-start.14 = (f32[1,4096]{1,0:T(1,128)S(1)}, f32[1,4096]{1,0:T(1,128)S(1)}, u32[]{:S(2)}, u32[]{:S(2)}) collective-permute-start(f32[1,4096]{1,0:T(1,128)S(1)} %get-tuple-element.118), channel_id=1, source_target_pairs={{0,1},{1,2},{2,3},{3,4},{4,5},{5,6},{6,7},{7,8},{8,9},{9,10},{10,1... | collective-permute-start | bytes 49160 | tf_op jit(solution)/shard_map/ppermute | solution.py:14
  78.0 9.5 %collective-permute-start.15 = (f32[1,4096]{1,0:T(1,128)S(1)}, f32[1,4096]{1,0:T(1,128)S(1)}, u32[]{:S(2)}, u32[]{:S(2)}) collective-permute-start(f32[1,4096]{1,0:T(1,128)S(1)} %get-tuple-element.115), channel_id=1, source_target_pairs={{1,0},{2,1},{3,2},{4,3},{5,4},{6,5},{7,6},{8,7},{9,8},{10,9},{11,1... | collective-permute-start | bytes 49160 | tf_op jit(solution)/shard_map/ppermute | solution.py:15
  80.0 9.0 %collective-permute-start.16 = (f32[1,4096]{1,0:T(1,128)S(1)}, f32[1,4096]{1,0:T(1,128)S(1)}, u32[]{:S(2)}, u32[]{:S(2)}) collective-permute-start(f32[1,4096]{1,0:T(1,128)S(1)} %get-tuple-element.116), channel_id=1, source_target_pairs={{0,1},{1,2},{2,3},{3,4},{4,5},{5,6},{6,7},{7,8},{8,9},{9,10},{10,1... | collective-permute-start | bytes 49160 | tf_op jit(solution)/shard_map/ppermute | solution.py:14
  90.5 9.5 %collective-permute-start.17 = (f32[1,4096]{1,0:T(1,128)S(1)}, f32[1,4096]{1,0:T(1,128)S(1)}, u32[]{:S(2)}, u32[]{:S(2)}) collective-permute-start(f32[1,4096]{1,0:T(1,128)S(1)} %get-tuple-element.113), channel_id=1, source_target_pairs={{1,0},{2,1},{3,2},{4,3},{5,4},{6,5},{7,6},{8,7},{9,8},{10,9},{11,1... | collective-permute-start | bytes 49160 | tf_op jit(solution)/shard_map/ppermute | solution.py:15
  92.4 9.0 %collective-permute-start.18 = (f32[1,4096]{1,0:T(1,128)S(1)}, f32[1,4096]{1,0:T(1,128)S(1)}, u32[]{:S(2)}, u32[]{:S(2)}) collective-permute-start(f32[1,4096]{1,0:T(1,128)S(1)} %get-tuple-element.114), channel_id=1, source_target_pairs={{0,1},{1,2},{2,3},{3,4},{4,5},{5,6},{6,7},{7,8},{8,9},{9,10},{10,1... | collective-permute-start | bytes 49160 | tf_op jit(solution)/shard_map/ppermute | solution.py:14
  102.9 72.1 %collective-permute-start.19 = (f32[1,4096]{1,0:T(1,128)S(1)}, f32[1,4096]{1,0:T(1,128)S(1)}, u32[]{:S(2)}, u32[]{:S(2)}) collective-permute-start(f32[1,4096]{1,0:T(1,128)S(1)} %get-tuple-element.111), channel_id=1, source_target_pairs={{1,0},{2,1},{3,2},{4,3},{5,4},{6,5},{7,6},{8,7},{9,8},{10,9},{11,1... | collective-permute-start | bytes 49160 | tf_op jit(solution)/shard_map/ppermute | solution.py:15
  104.9 70.2 %collective-permute-start.20 = (f32[1,4096]{1,0:T(1,128)S(1)}, f32[1,4096]{1,0:T(1,128)S(1)}, u32[]{:S(2)}, u32[]{:S(2)}) collective-permute-start(f32[1,4096]{1,0:T(1,128)S(1)} %get-tuple-element.112), channel_id=1, source_target_pairs={{0,1},{1,2},{2,3},{3,4},{4,5},{5,6},{6,7},{7,8},{8,9},{9,10},{10,1... | collective-permute-start | bytes 49160 | tf_op jit(solution)/shard_map/ppermute | solution.py:14
  175.4 7.7 %collective-permute-start.21 = (f32[16,4096]{1,0:T(8,128)S(1)}, f32[16,4096]{1,0:T(8,128)S(1)}, u32[]{:S(2)}, u32[]{:S(2)}) collective-permute-start(f32[16,4096]{1,0:T(8,128)S(1)} %fusion.19), channel_id=1, source_target_pairs={{0,32},{32,64},{64,96},{96,128},{128,160},{160,192},{192,224},{1,3... | collective-permute-start | bytes 786440 | tf_op jit(solution)/shard_map/ppermute | solution.py:23
  214.9 5.9 %collective-permute-start = (f32[1,2048]{1,0:T(1,128)S(1)}, f32[1,2048]{1,0:T(1,128)S(1)}, u32[]{:S(2)}, u32[]{:S(2)}) collective-permute-start(f32[1,2048]{1,0:T(1,128)S(1)} %get-tuple-element.168), channel_id=1, source_target_pairs={{0,1},{1,2},{2,3},{3,4},{4,5},{5,6},{6,7},{7,8},{8,9},{9,10},{10,1... | collective-permute-start | bytes 24584 | tf_op jit(solution)/shard_map/while/body/eval_jaxpr/ppermute | solution.py:14
  218.9 8.9 %collective-permute-start.1 = (f32[1,2048]{1,0:T(1,128)S(1)}, f32[1,2048]{1,0:T(1,128)S(1)}, u32[]{:S(2)}, u32[]{:S(2)}) collective-permute-start(f32[1,2048]{1,0:T(1,128)S(1)} %get-tuple-element.169), channel_id=1, source_target_pairs={{1,0},{2,1},{3,2},{4,3},{5,4},{6,5},{7,6},{8,7},{9,8},{10,9},{11,1... | collective-permute-start | bytes 24584 | tf_op jit(solution)/shard_map/while/body/eval_jaxpr/ppermute | solution.py:15
  233.5 5.9 %collective-permute-start = (f32[1,2048]{1,0:T(1,128)S(1)}, f32[1,2048]{1,0:T(1,128)S(1)}, u32[]{:S(2)}, u32[]{:S(2)}) collective-permute-start(f32[1,2048]{1,0:T(1,128)S(1)} %get-tuple-element.168), channel_id=1, source_target_pairs={{0,1},{1,2},{2,3},{3,4},{4,5},{5,6},{6,7},{7,8},{8,9},{9,10},{10,1... | collective-permute-start | bytes 24584 | tf_op jit(solution)/shard_map/while/body/eval_jaxpr/ppermute | solution.py:14
  235.4 8.9 %collective-permute-start.1 = (f32[1,2048]{1,0:T(1,128)S(1)}, f32[1,2048]{1,0:T(1,128)S(1)}, u32[]{:S(2)}, u32[]{:S(2)}) collective-permute-start(f32[1,2048]{1,0:T(1,128)S(1)} %get-tuple-element.169), channel_id=1, source_target_pairs={{1,0},{2,1},{3,2},{4,3},{5,4},{6,5},{7,6},{8,7},{9,8},{10,9},{11,1... | collective-permute-start | bytes 24584 | tf_op jit(solution)/shard_map/while/body/eval_jaxpr/ppermute | solution.py:15
  250.0 5.9 %collective-permute-start = (f32[1,2048]{1,0:T(1,128)S(1)}, f32[1,2048]{1,0:T(1,128)S(1)}, u32[]{:S(2)}, u32[]{:S(2)}) collective-permute-start(f32[1,2048]{1,0:T(1,128)S(1)} %get-tuple-element.168), channel_id=1, source_target_pairs={{0,1},{1,2},{2,3},{3,4},{4,5},{5,6},{6,7},{7,8},{8,9},{9,10},{10,1... | collective-permute-start | bytes 24584 | tf_op jit(solution)/shard_map/while/body/eval_jaxpr/ppermute | solution.py:14
  252.0 8.9 %collective-permute-start.1 = (f32[1,2048]{1,0:T(1,128)S(1)}, f32[1,2048]{1,0:T(1,128)S(1)}, u32[]{:S(2)}, u32[]{:S(2)}) collective-permute-start(f32[1,2048]{1,0:T(1,128)S(1)} %get-tuple-element.169), channel_id=1, source_target_pairs={{1,0},{2,1},{3,2},{4,3},{5,4},{6,5},{7,6},{8,7},{9,8},{10,9},{11,1... | collective-permute-start | bytes 24584 | tf_op jit(solution)/shard_map/while/body/eval_jaxpr/ppermute | solution.py:15
  266.6 5.9 %collective-permute-start = (f32[1,2048]{1,0:T(1,128)S(1)}, f32[1,2048]{1,0:T(1,128)S(1)}, u32[]{:S(2)}, u32[]{:S(2)}) collective-permute-start(f32[1,2048]{1,0:T(1,128)S(1)} %get-tuple-element.168), channel_id=1, source_target_pairs={{0,1},{1,2},{2,3},{3,4},{4,5},{5,6},{6,7},{7,8},{8,9},{9,10},{10,1... | collective-permute-start | bytes 24584 | tf_op jit(solution)/shard_map/while/body/eval_jaxpr/ppermute | solution.py:14
  268.5 8.9 %collective-permute-start.1 = (f32[1,2048]{1,0:T(1,128)S(1)}, f32[1,2048]{1,0:T(1,128)S(1)}, u32[]{:S(2)}, u32[]{:S(2)}) collective-permute-start(f32[1,2048]{1,0:T(1,128)S(1)} %get-tuple-element.169), channel_id=1, source_target_pairs={{1,0},{2,1},{3,2},{4,3},{5,4},{6,5},{7,6},{8,7},{9,8},{10,9},{11,1... | collective-permute-start | bytes 24584 | tf_op jit(solution)/shard_map/while/body/eval_jaxpr/ppermute | solution.py:15
  283.2 5.9 %collective-permute-start = (f32[1,2048]{1,0:T(1,128)S(1)}, f32[1,2048]{1,0:T(1,128)S(1)}, u32[]{:S(2)}, u32[]{:S(2)}) collective-permute-start(f32[1,2048]{1,0:T(1,128)S(1)} %get-tuple-element.168), channel_id=1, source_target_pairs={{0,1},{1,2},{2,3},{3,4},{4,5},{5,6},{6,7},{7,8},{8,9},{9,10},{10,1... | collective-permute-start | bytes 24584 | tf_op jit(solution)/shard_map/while/body/eval_jaxpr/ppermute | solution.py:14
  285.1 8.9 %collective-permute-start.1 = (f32[1,2048]{1,0:T(1,128)S(1)}, f32[1,2048]{1,0:T(1,128)S(1)}, u32[]{:S(2)}, u32[]{:S(2)}) collective-permute-start(f32[1,2048]{1,0:T(1,128)S(1)} %get-tuple-element.169), channel_id=1, source_target_pairs={{1,0},{2,1},{3,2},{4,3},{5,4},{6,5},{7,6},{8,7},{9,8},{10,9},{11,1... | collective-permute-start | bytes 24584 | tf_op jit(solution)/shard_map/while/body/eval_jaxpr/ppermute | solution.py:15
  301.6 8.9 %collective-permute-start.1 = (f32[1,2048]{1,0:T(1,128)S(1)}, f32[1,2048]{1,0:T(1,128)S(1)}, u32[]{:S(2)}, u32[]{:S(2)}) collective-permute-start(f32[1,2048]{1,0:T(1,128)S(1)} %get-tuple-element.169), channel_id=1, source_target_pairs={{1,0},{2,1},{3,2},{4,3},{5,4},{6,5},{7,6},{8,7},{9,8},{10,9},{11,1... | collective-permute-start | bytes 24584 | tf_op jit(solution)/shard_map/while/body/eval_jaxpr/ppermute | solution.py:15
  316.3 5.9 %collective-permute-start = (f32[1,2048]{1,0:T(1,128)S(1)}, f32[1,2048]{1,0:T(1,128)S(1)}, u32[]{:S(2)}, u32[]{:S(2)}) collective-permute-start(f32[1,2048]{1,0:T(1,128)S(1)} %get-tuple-element.168), channel_id=1, source_target_pairs={{0,1},{1,2},{2,3},{3,4},{4,5},{5,6},{6,7},{7,8},{8,9},{9,10},{10,1... | collective-permute-start | bytes 24584 | tf_op jit(solution)/shard_map/while/body/eval_jaxpr/ppermute | solution.py:14
  318.2 8.9 %collective-permute-start.1 = (f32[1,2048]{1,0:T(1,128)S(1)}, f32[1,2048]{1,0:T(1,128)S(1)}, u32[]{:S(2)}, u32[]{:S(2)}) collective-permute-start(f32[1,2048]{1,0:T(1,128)S(1)} %get-tuple-element.169), channel_id=1, source_target_pairs={{1,0},{2,1},{3,2},{4,3},{5,4},{6,5},{7,6},{8,7},{9,8},{10,9},{11,1... | collective-permute-start | bytes 24584 | tf_op jit(solution)/shard_map/while/body/eval_jaxpr/ppermute | solution.py:15
  (12 other events, 126.1 us)
where the time goes:
time: 337 us; the launch traced here: 335 us
  starting transfers between devices  138 us (41%)
  waiting for transfers between devices  82.8 us (25%)
  local copies, waits for them, and re-layouts  73.1 us (22%)
  other arithmetic  40.1 us (12%)
    ppermute x15, starting transfers between devices, padded(): before = lax.ppermute(last, axis, up)  75.4 us
    reshape x2, local copies, waits for them, and re-layouts, restrict(): field.reshape(lead + (field.shape[-2] // 2, 2, field.shape[-1] // 2, 2))  68.3 us
    ppermute x15, starting transfers between devices, padded(): after = lax.ppermute(leading, axis, down)  40.8 us
    ppermute x10, waiting for transfers between devices, from_behind(): lax.ppermute(value, axis, [(source, source + steps) for source in range(l...  36.7 us
    ppermute x15, waiting for transfers between devices, padded(): after = lax.ppermute(leading, axis, down)  36.4 us
    reduce_sum x2, other arithmetic, restrict(): return jnp.mean(shaped, axis=(-3, -1))  24.4 us
    ppermute x10, starting transfers between devices, from_behind(): lax.ppermute(value, axis, [(source, source + steps) for source in range(l...  22.2 us
    add x8, other arithmetic, propagate(): field = interior(extended, cond_rows, cond_cols) + source_rows  11.7 us
  transfers between devices with their start and end apart: 40, of which 23 were waited for; matrix products, arithmetic and copies ran while one was open for 19% of the time, Pallas kernels for 0%

commit v1 on v0

v1 whole, which is shorter than its diff:
```python
import functools

import jax
import jax.numpy as jnp
from jax import lax
from jax.experimental import pallas as pl
from jax.experimental.pallas import tpu as pltpu
from jax.sharding import PartitionSpec as P

MESH = pl.DeviceIdType.MESH
F32 = jnp.float32
L = 128
TOP = 16


def remote(src, dst, send, recv, where):
    return pltpu.make_async_remote_copy(
        src_ref=src, dst_ref=dst, send_sem=send, recv_sem=recv, device_id=where, device_id_type=MESH
    )


def lane_index():
    return lax.broadcasted_iota(jnp.int32, (8, L), 1)


def gather_lanes(value, index):
    return jnp.take_along_axis(value, index, axis=1, mode="promise_in_bounds")


def restrict_block(ref, block, row, lane):
    halves = []
    for q in range(2):
        pair = ref[2 * block + q, pl.ds(row, 8, stride=2), :] + ref[
            2 * block + q, pl.ds(row + 1, 8, stride=2), :
        ]
        pair = pair + pltpu.roll(pair, L - 1, 1)
        halves.append(gather_lanes(pair, (2 * lane) % L))
    return jnp.where(lane < L // 2, halves[0], halves[1]) * 0.25


def fluxes(u, right, up, down, cx, cx_up, cy, carry, lane):
    flow = cy * (right - u)
    turned = pltpu.roll(flow, 1, 1)
    west = jnp.where(lane == 0, carry, turned)
    total = cx * (down - u) - cx_up * (u - up)
    return total + flow - west, turned


def fine_step(src, dst, cx, cy, source, first, tiles, last_strip, blocks, unroll=4):
    lane = lane_index()
    row = lax.broadcasted_iota(jnp.int32, (8, L), 0)
    rows = [first + 8 * k for k in range(tiles)]
    outside = [None if r + 8 <= TOP + 16 else (row + r >= TOP + 16) & last_strip for r in rows]

    def body(b, carry):
        new = []
        for k, r in enumerate(rows):
            u, ru, turned = carry[k]
            nxt = src[b + 1, r : r + 8, :]
            rn = pltpu.roll(nxt, L - 1, 1)
            right = jnp.where(lane == L - 1, rn, ru)
            change, turned = fluxes(
                u, right, src[b, r - 1 : r + 7, :], src[b, r + 1 : r + 9, :],
                cx[b, r : r + 8, :], cx[b, r - 1 : r + 7, :], cy[b, r : r + 8, :], turned, lane,
            )
            out = u + change + source[b, r : r + 8, :]
            if outside[k] is not None:
                out = jnp.where(outside[k], 0.0, out)
            dst[b, r : r + 8, :] = out
            new.append((nxt, rn, turned))
        return tuple(new)

    start = []
    for r in rows:
        u = src[0, r : r + 8, :]
        start.append((u, pltpu.roll(u, L - 1, 1), jnp.zeros((8, L), F32)))
    lax.fori_loop(0, blocks, body, tuple(start), unroll=unroll)


def kernel(
    groups, strips, guess_in, cx_in, cy_in, source_in, inflow_in, out_hbm,
    stage, flow_stage, own, u0, u1, u2, cx, cy, source, rcx, rcy, inflow, tcoarse, dwin,
    wsrc, win, fa, fb, rd, fsend, frecv, out,
    in_sems, out_sem, a_send, a_recv, w_send, w_recv, d_send, d_recv, f_send, f_recv,
):
    t = lax.axis_index("tm")
    s = lax.axis_index("space")
    even = lax.rem(t, 2) == 0
    has_up, has_down = s > 0, s < strips - 1
    last_t = groups - 1
    lane = lane_index()
    zero = jnp.zeros((8, L), F32)

    loads = [
        pltpu.make_async_copy(ref, stage.at[i], in_sems.at[i])
        for i, ref in enumerate((guess_in.at[0], cx_in, cy_in, source_in))
    ]
    loads.append(pltpu.make_async_copy(inflow_in, flow_stage, in_sems.at[4]))
    for load in loads:
        load.start()

    barrier = pltpu.get_barrier_semaphore()
    for k in range(1, groups):
        pl.semaphore_signal(barrier, inc=1, device_id=(lax.rem(t + k, groups), s), device_id_type=MESH)

    @pl.when(has_up)
    def _():
        for k in range(groups):
            pl.semaphore_signal(barrier, inc=1, device_id=(lax.rem(t + k, groups), s - 1), device_id_type=MESH)

    @pl.when(has_down)
    def _():
        for k in range(groups):
            pl.semaphore_signal(barrier, inc=1, device_id=(lax.rem(t + k, groups), s + 1), device_id_type=MESH)

    near = 3 - jnp.where(has_up, 0, 1) - jnp.where(has_down, 0, 1)

    for load in loads:
        load.wait()
    blocks = own.shape[0]
    cblocks = blocks // 2
    for b in range(blocks):
        cols = slice(b * L, (b + 1) * L)
        own[b, :, :] = stage[0, :, cols]
        cx[b, TOP : TOP + 16, :] = stage[1, :, cols]
        cy[b, TOP : TOP + 16, :] = stage[2, :, cols]
        source[b, TOP : TOP + 16, :] = stage[3, :, cols]
    pl.semaphore_wait(barrier, groups * near - 1)

    up_rows, down_rows, main_rows = slice(TOP - 8, TOP), slice(TOP + 16, TOP + 24), slice(TOP, TOP + 16)
    ahead = lax.rem(t + 1, groups)
    mate = jnp.where(even, t + 1, t - 1)
    coefs = (cx, cy, source)
    sends = []
    inner = u0.at[0:blocks]

    def send(cond, copy):
        sends.append((cond, copy))

        @pl.when(cond)
        def _():
            copy.start()

    for i, ref in enumerate(coefs):
        send(even & has_down, remote(ref.at[:, TOP + 8 : TOP + 16, :], ref.at[:, up_rows, :], a_send.at[i], a_recv.at[i], (t, s + 1)))
        send(~even & has_up, remote(ref.at[:, TOP : TOP + 8, :], ref.at[:, down_rows, :], a_send.at[3 + i], a_recv.at[3 + i], (t, s - 1)))
    guess_down, guess_up = own.at[:, 8:16, :], own.at[:, 0:8, :]
    send((t < last_t) & has_down, remote(guess_down, inner.at[:, up_rows, :], a_send.at[6], a_recv.at[6], (ahead, s + 1)))
    send((t < last_t) & has_up, remote(guess_up, inner.at[:, down_rows, :], a_send.at[7], a_recv.at[7], (ahead, s - 1)))
    send(t < last_t, remote(own, inner.at[:, main_rows, :], a_send.at[8], a_recv.at[8], (ahead, s)))
    send((t == 0) & has_down, remote(guess_down, inner.at[:, up_rows, :], a_send.at[9], a_recv.at[6], (t, s + 1)))
    send((t == 0) & has_up, remote(guess_up, inner.at[:, down_rows, :], a_send.at[10], a_recv.at[7], (t, s - 1)))

    for ref in (rcx, rcy, inflow):
        rows = ref.shape[1]
        for r in range(0, rows, 8):
            ref[0, r : r + 8, :] = zero
            ref[cblocks + 1, r : r + 8, :] = zero
    for b in range(cblocks):
        inflow[b + 1, :, :] = flow_stage[:, b * L : (b + 1) * L]

    def coarse_coefs(b, c):
        rcx[b + 1, 8:16, :] = restrict_block(cx, b, TOP, lane)
        rcy[b + 1, 8:16, :] = restrict_block(cy, b, TOP, lane)
        return c

    lax.fori_loop(0, cblocks, coarse_coefs, 0)

    def shifted(ref, rows):
        turned = [pltpu.roll(ref[2 * t + i, rows, :], L // 2, 1) for i in range(4)]
        return [jnp.where(lane < L // 2, turned[i], turned[i + 1]) for i in range(3)]

    for a, (ref, rows) in enumerate(((inflow, slice(0, 8)), (rcx, slice(8, 16)), (rcy, slice(8, 16)))):
        for i, value in enumerate(shifted(ref, rows)):
            wsrc[a, i, :, :] = value
            win[a, i, 16:24, :] = value
    send(has_down, remote(wsrc, win.at[:, :, 8:16, :], w_send.at[0], w_recv.at[0], (t, s + 1)))
    send(has_up, remote(wsrc, win.at[:, :, 24:32, :], w_send.at[1], w_recv.at[1], (t, s - 1)))

    def clear(ref, rows):
        def body(b, c):
            ref[b, rows, :] = zero
            return c

        lax.fori_loop(0, ref.shape[0], body, 0)

    for ref in (u0, u1, u2):
        for r in range(0, ref.shape[1], 8):
            ref[blocks, r : r + 8, :] = zero

    @pl.when(~has_up)
    def _():
        for ref in (cx, cy, source):
            clear(ref, up_rows)
        clear(inner, up_rows)
        for i in range(3):
            for a in range(3):
                win[a, i, 8:16, :] = zero
            for j in range(last_t):
                rd[j, i, 0:8, :] = zero

    @pl.when(~has_down)
    def _():
        for ref in (cx, cy, source):
            clear(ref, down_rows)
        clear(inner, down_rows)
        for i in range(3):
            for a in range(3):
                win[a, i, 24:32, :] = zero
            for j in range(last_t):
                rd[j, i, 16:24, :] = zero

    @pl.when(t == 0)
    def _():
        for b in range(blocks):
            u0[b, main_rows, :] = own[b, :, :]

    for i, ref in enumerate(coefs):
        upper, lower = ref.at[:, up_rows, :], ref.at[:, down_rows, :]
        up_copy = remote(upper, upper, a_send.at[11 + i], a_recv.at[i], (mate, s))
        down_copy = remote(lower, lower, a_send.at[14 + i], a_recv.at[3 + i], (mate, s))

        @pl.when(even & has_up)
        def _(up_copy=up_copy):
            up_copy.wait_recv()

        send(even & has_up, up_copy)

        @pl.when(~even & has_down)
        def _(down_copy=down_copy):
            down_copy.wait_recv()

        send(~even & has_down, down_copy)

        @pl.when(~even & has_up)
        def _(up_copy=up_copy):
            up_copy.wait_recv()

        @pl.when(even & has_down)
        def _(down_copy=down_copy):
            down_copy.wait_recv()

    @pl.when(has_up)
    def _():
        remote(guess_down, inner.at[:, up_rows, :], a_send.at[6], a_recv.at[6], (t, s)).wait_recv()

    @pl.when(has_down)
    def _():
        remote(guess_up, inner.at[:, down_rows, :], a_send.at[7], a_recv.at[7], (t, s)).wait_recv()

    @pl.when(t > 0)
    def _():
        remote(own, inner.at[:, main_rows, :], a_send.at[8], a_recv.at[8], (t, s)).wait_recv()

    step = functools.partial(fine_step, cx=cx, cy=cy, source=source, last_strip=~has_down, blocks=blocks)

    @pl.when(t > 0)
    def _():
        def pair(i, c):
            step(u0, u1, first=TOP - 8, tiles=4)
            step(u1, u0, first=TOP - 8, tiles=4)
            return c

        lax.fori_loop(0, 2, pair, 0)

    def coarse_relaxed(b, c):
        rcx[b + 1, 0:8, :] = restrict_block(cx, b, 0, lane)
        for k in range(3):
            value = restrict_block(u0, b, 16 * k, lane)
            tcoarse[b, 8 * k : 8 * k + 8, :] = jnp.where(t > 0, value, 0.0)
        return c

    lax.fori_loop(0, cblocks, coarse_relaxed, 0)
    for r in range(0, 24, 8):
        tcoarse[cblocks, r : r + 8, :] = zero

    @pl.when(~has_down)
    def _():
        def body(b, c):
            tcoarse[b, 16:24, :] = zero
            return c

        lax.fori_loop(0, cblocks, body, 0)

    @pl.when(t < last_t)
    def _():
        step(u0, u1, first=TOP - 4, tiles=3)
        step(u1, u2, first=TOP - 4, tiles=3)
        step(u2, u1, first=TOP - 4, tiles=3)
        step(u1, u2, first=TOP, tiles=2)

        def body(b, carry):
            u, ru, turned, before = carry
            nxt = tcoarse[b + 1, 8:16, :]
            rn = pltpu.roll(nxt, L - 1, 1)
            right = jnp.where(lane == L - 1, rn, ru)
            change, turned = fluxes(
                u, right, tcoarse[b, 7:15, :], tcoarse[b, 9:17, :],
                rcx[b + 1, 8:16, :], rcx[b + 1, 7:15, :], rcy[b + 1, 8:16, :], turned, lane,
            )
            value = restrict_block(u2, b, TOP, lane) - (u + change)
            value = pltpu.roll(value, L // 2, 1)
            dwin[b, :, :] = jnp.where(lane < L // 2, before, value)
            return nxt, rn, turned, value

        u = tcoarse[0, 8:16, :]
        carry = lax.fori_loop(0, cblocks, body, (u, pltpu.roll(u, L - 1, 1), zero, zero))
        dwin[cblocks, :, :] = jnp.where(lane < L // 2, carry[3], 0.0)

    for k in range(groups):
        c = lax.rem(t + k, groups)
        piece = dwin.at[pl.ds(2 * c, 3)]
        if k == 0:
            @pl.when(t < last_t)
            def _():
                for i in range(3):
                    rd[t, i, 8:16, :] = dwin[2 * t + i, :, :]
        else:
            send(t < last_t, remote(piece, rd.at[t, :, 8:16, :], d_send.at[k, 1], d_recv.at[t, 1], (c, s)))
        send((t < last_t - 1) & has_down, remote(piece, rd.at[t, :, 0:8, :], d_send.at[k, 0], d_recv.at[t, 0], (c, s + 1)))
        send((t < last_t - 1) & has_up, remote(piece, rd.at[t, :, 16:24, :], d_send.at[k, 2], d_recv.at[t, 2], (c, s - 1)))

    @pl.when(has_up)
    def _():
        remote(wsrc, win.at[:, :, 8:16, :], w_send.at[0], w_recv.at[0], (t, s)).wait_recv()

    @pl.when(has_down)
    def _():
        remote(wsrc, win.at[:, :, 24:32, :], w_send.at[1], w_recv.at[1], (t, s)).wait_recv()

    row = lax.broadcasted_iota(jnp.int32, (8, L), 0)
    keep = {}
    for k in range(3):
        for i in range(3):
            bad = None
            if k == 2:
                bad = jnp.broadcast_to(~has_down, (8, L))
            if i == 2:
                beyond = (lane >= L // 2) & (t == last_t)
                bad = beyond if bad is None else bad | beyond
            keep[k, i] = bad
    for i in range(3):
        for k in range(3):
            fa[i, 8 + 8 * k : 16 + 8 * k, :] = win[0, i, 8 + 8 * k : 16 + 8 * k, :]
    now, later = fa, fb
    for g in range(1, groups):
        j = g - 1
        piece = dwin.at[pl.ds(0, 3)]

        @pl.when(t != j)
        def _():
            remote(piece, rd.at[j, :, 8:16, :], d_send.at[0, 1], d_recv.at[j, 1], (t, s)).wait_recv()

        if j < last_t - 1:
            @pl.when(has_up)
            def _():
                remote(piece, rd.at[j, :, 0:8, :], d_send.at[0, 0], d_recv.at[j, 0], (t, s)).wait_recv()

            @pl.when(has_down)
            def _():
                remote(piece, rd.at[j, :, 16:24, :], d_send.at[0, 2], d_recv.at[j, 2], (t, s)).wait_recv()

        middle = []
        for k in range(3):
            if j == last_t - 1 and k != 1:
                continue
            r = 8 + 8 * k
            turned = zero
            for i in range(3):
                u = now[i, r : r + 8, :]
                ru = pltpu.roll(u, L - 1, 1)
                rn = pltpu.roll(now[i + 1, r : r + 8, :], L - 1, 1) if i < 2 else zero
                right = jnp.where(lane == L - 1, rn, ru)
                change, turned = fluxes(
                    u, right, now[i, r - 1 : r + 7, :], now[i, r + 1 : r + 9, :],
                    win[1, i, r : r + 8, :], win[1, i, r - 1 : r + 7, :], win[2, i, r : r + 8, :], turned, lane,
                )
                value = u + change + rd[j, i, 8 * k : 8 * k + 8, :]
                if keep[k, i] is not None:
                    value = jnp.where(keep[k, i], 0.0, value)
                later[i, r : r + 8, :] = value
                if k == 1:
                    middle.append(pltpu.roll(value, L // 2, 1))
        for i in range(2):
            fsend[g, i, :, :] = jnp.where(lane < L // 2, middle[i], middle[i + 1])

        @pl.when(t == g)
        def _():
            for i in range(2):
                frecv[2 * t + i, :, :] = fsend[g, i, :, :]

        send(t != g, remote(fsend.at[g], frecv.at[pl.ds(2 * t, 2)], f_send.at[g], f_recv.at[t], (g, s)))
        now, later = later, now

    @pl.when(t == 0)
    def _():
        for b in range(cblocks):
            frecv[b, :, :] = inflow[b + 1, :, :]

    for c in range(groups):
        @pl.when((t > 0) & (t != c))
        def _():
            remote(fsend.at[0], frecv.at[pl.ds(2 * c, 2)], f_send.at[0], f_recv.at[c], (t, s)).wait_recv()

        for i in range(2):
            b = 2 * c + i
            error = frecv[b, :, :] - tcoarse[b, 8:16, :]
            for q in range(2):
                wide = gather_lanes(error, lane // 2 + q * (L // 2))
                f = 2 * b + q
                for p in range(2):
                    tall = jnp.take_along_axis(wide, row // 2 + 4 * p, axis=0, mode="promise_in_bounds")
                    out[8 * p : 8 * p + 8, f * L : (f + 1) * L] = tall + u0[f, TOP + 8 * p : TOP + 8 * p + 8, :]
    store = pltpu.make_async_copy(out, out_hbm.at[0], out_sem)
    store.start()
    for cond, copy in sends:
        @pl.when(cond)
        def _(copy=copy):
            copy.wait_send()
    store.wait()


def solution(mesh):
    groups, strips = mesh.shape["tm"], mesh.shape["space"]

    def shards(guesses, cond_x, cond_y, source, inflow):
        _, rows, columns = guesses.shape
        blocks = columns // L
        assert rows == 16
        cblocks = blocks // 2
        vmem = lambda *shape: pltpu.VMEM(shape, F32)
        dma = lambda *shape: pltpu.SemaphoreType.DMA(shape)
        return pl.pallas_call(
            functools.partial(kernel, groups, strips),
            out_shape=jax.ShapeDtypeStruct(guesses.shape, F32),
            in_specs=[pl.BlockSpec(memory_space=pl.ANY)] * 5,
            out_specs=pl.BlockSpec(memory_space=pl.ANY),
            scratch_shapes=[
                vmem(4, rows, columns), vmem(rows // 2, columns // 2), vmem(blocks, rows, L),
                vmem(blocks + 1, 48, L), vmem(blocks + 1, 48, L), vmem(blocks + 1, 48, L),
                vmem(blocks, 48, L), vmem(blocks, 48, L), vmem(blocks, 48, L),
                vmem(cblocks + 2, 24, L), vmem(cblocks + 2, 24, L), vmem(cblocks + 2, 8, L),
                vmem(cblocks + 1, 24, L), vmem(cblocks + 1, 8, L),
                vmem(3, 3, 8, L), vmem(3, 3, 40, L), vmem(3, 40, L), vmem(3, 40, L),
                vmem(groups - 1, 3, 24, L), vmem(groups, 2, 8, L), vmem(cblocks, 8, L), vmem(rows, columns),
                dma(5), pltpu.SemaphoreType.DMA, dma(17), dma(9), dma(2), dma(2),
                dma(groups, 3), dma(groups, 3), dma(groups), dma(groups),
            ],
            compiler_params=pltpu.CompilerParams(
                collective_id=0, has_side_effects=True, vmem_limit_bytes=40 * 2**20
            ),
        )(guesses, cond_x, cond_y, source, inflow)

    return jax.shard_map(
        shards,
        mesh=mesh,
        in_specs=(
            P("tm", "space", None),
            P("space", None),
            P("space", None),
            P("space", None),
            P("space", None),
        ),
        out_specs=P("tm", "space", None),
        check_vma=False,
    )
```

time: 337 us -> 51 us (0.15)
  the two profiles are of different devices: /device:TPU:122 before, /device:TPU:135 now
where the time goes in v1:
time: 51 us; the launch traced here: 50.8 us
  Pallas kernels  45.4 us (89%)
  local copies, waits for them, and re-layouts  5.34 us (10%)
    pallas_call x1, Pallas kernels, shards(): pl.pallas_call(functools.partial(kernel, groups, strips), out_shape=jax.S...  45.4 us
    unnamed x11, local copies, waits for them, and re-layouts  5.34 us

profile of v1, /device:TPU:135, one launch (start us, length us, event | category | flops | bytes accessed | tf_op | source)
XLA Modules:
  0.0 50.8 jit_solution(6117341202474399440)
XLA Ops:
  0.0 0.0 copy-start
  0.0 0.9 %copy-done = f32[1,16,4096]{2,1,0:T(8,128)S(1)} copy-done((f32[1,16,4096]{2,1,0:T(8,128)S(1)}, f32[1,16,4096]{2,1,0:T(8,128)}, u32[]{:S(2)}) %copy-start) | copy-done | bytes 262168
  1.0 0.0 copy-start.1
  1.0 0.9 %copy-done.1 = f32[16,4096]{1,0:T(8,128)S(1)} copy-done((f32[16,4096]{1,0:T(8,128)S(1)}, f32[16,4096]{1,0:T(8,128)}, u32[]{:S(2)}) %copy-start.1) | copy-done | bytes 262168
  1.9 0.0 copy-start.2
  1.9 0.9 %copy-done.2 = f32[16,4096]{1,0:T(8,128)S(1)} copy-done((f32[16,4096]{1,0:T(8,128)S(1)}, f32[16,4096]{1,0:T(8,128)}, u32[]{:S(2)}) %copy-start.2) | copy-done | bytes 262168
  2.9 0.0 copy-start.3
  2.9 0.9 %copy-done.3 = f32[16,4096]{1,0:T(8,128)S(1)} copy-done((f32[16,4096]{1,0:T(8,128)S(1)}, f32[16,4096]{1,0:T(8,128)}, u32[]{:S(2)}) %copy-start.3) | copy-done | bytes 262168
  3.8 0.0 copy-start.4
  3.8 0.8 %copy-done.4 = f32[8,2048]{1,0:T(8,128)S(1)} copy-done((f32[8,2048]{1,0:T(8,128)S(1)}, f32[8,2048]{1,0:T(8,128)}, u32[]{:S(2)}) %copy-start.4) | copy-done | bytes 65560
  4.6 45.4 %shard_map.55 = f32[1,16,4096]{2,1,0:T(8,128)S(1)} custom-call(f32[1,16,4096]{2,1,0:T(8,128)S(1)} %copy-done, f32[16,4096]{1,0:T(8,128)S(1)} %copy-done.1, f32[16,4096]{1,0:T(8,128)S(1)} %copy-done.2, f32[16,4096]{1,0:T(8,128)S(1)} %copy-done.3, f32[8,2048]{1,0:T(8,128)S(1)} %copy-done.4), custom_call_target="tpu_custom_call" | custom-call | tf_op jit(solution)/shard_map/pallas_call | solution.py:433
  50.1 0.7 %copy.7 = f32[1,16,4096]{2,1,0:T(8,128)} copy(f32[1,16,4096]{2,1,0:T(8,128)S(1)} %shard_map.55) | data formatting | bytes 524288
Async XLA Ops:
  0.0 0.9 %copy-start = (f32[1,16,4096]{2,1,0:T(8,128)S(1)}, f32[1,16,4096]{2,1,0:T(8,128)}, u32[]{:S(2)}) copy-start(f32[1,16,4096]{2,1,0:T(8,128)} %guess_in.1) | copy-start | bytes 786436
  1.0 0.9 %copy-start.1 = (f32[16,4096]{1,0:T(8,128)S(1)}, f32[16,4096]{1,0:T(8,128)}, u32[]{:S(2)}) copy-start(f32[16,4096]{1,0:T(8,128)} %cx_in.1) | copy-start | bytes 786436
  1.9 0.9 %copy-start.2 = (f32[16,4096]{1,0:T(8,128)S(1)}, f32[16,4096]{1,0:T(8,128)}, u32[]{:S(2)}) copy-start(f32[16,4096]{1,0:T(8,128)} %cy_in.1) | copy-start | bytes 786436
  2.9 0.9 %copy-start.3 = (f32[16,4096]{1,0:T(8,128)S(1)}, f32[16,4096]{1,0:T(8,128)}, u32[]{:S(2)}) copy-start(f32[16,4096]{1,0:T(8,128)} %source_in.1) | copy-start | bytes 786436
  3.8 0.8 %copy-start.4 = (f32[8,2048]{1,0:T(8,128)S(1)}, f32[8,2048]{1,0:T(8,128)}, u32[]{:S(2)}) copy-start(f32[8,2048]{1,0:T(8,128)} %inflow_in.1) | copy-start | bytes 196612

commit v2 on v1

--- a/solution.py
+++ b/solution.py
@@ -46,7 +46,7 @@
     return total + flow - west, turned
 
 
-def fine_step(src, dst, cx, cy, source, first, tiles, last_strip, blocks, unroll=4):
+def fine_step(src, dst, cx, cy, source, first, tiles, last_strip, blocks, unroll=32):
     lane = lane_index()
     row = lax.broadcasted_iota(jnp.int32, (8, L), 0)
     rows = [first + 8 * k for k in range(tiles)]
@@ -91,6 +91,14 @@
     lane = lane_index()
     zero = jnp.zeros((8, L), F32)
 
+    sends = []
+
+    def drain():
+        for cond, copy in sends:
+            @pl.when(cond)
+            def _(copy=copy):
+                copy.wait_send()
+
     loads = [
         pltpu.make_async_copy(ref, stage.at[i], in_sems.at[i])
         for i, ref in enumerate((guess_in.at[0], cx_in, cy_in, source_in))
@@ -131,7 +139,6 @@
     ahead = lax.rem(t + 1, groups)
     mate = jnp.where(even, t + 1, t - 1)
     coefs = (cx, cy, source)
-    sends = []
     inner = u0.at[0:blocks]
 
     def send(cond, copy):
@@ -164,7 +171,7 @@
         rcy[b + 1, 8:16, :] = restrict_block(cy, b, TOP, lane)
         return c
 
-    lax.fori_loop(0, cblocks, coarse_coefs, 0)
+    lax.fori_loop(0, cblocks, coarse_coefs, 0, unroll=16)
 
     def shifted(ref, rows):
         turned = [pltpu.roll(ref[2 * t + i, rows, :], L // 2, 1) for i in range(4)]
@@ -252,6 +259,14 @@
     def _():
         remote(own, inner.at[:, main_rows, :], a_send.at[8], a_recv.at[8], (t, s)).wait_recv()
 
+    @pl.when(has_up)
+    def _():
+        remote(wsrc, win.at[:, :, 8:16, :], w_send.at[0], w_recv.at[0], (t, s)).wait_recv()
+
+    @pl.when(has_down)
+    def _():
+        remote(wsrc, win.at[:, :, 24:32, :], w_send.at[1], w_recv.at[1], (t, s)).wait_recv()
+
     step = functools.partial(fine_step, cx=cx, cy=cy, source=source, last_strip=~has_down, blocks=blocks)
 
     @pl.when(t > 0)
@@ -270,7 +285,7 @@
             tcoarse[b, 8 * k : 8 * k + 8, :] = jnp.where(t > 0, value, 0.0)
         return c
 
-    lax.fori_loop(0, cblocks, coarse_relaxed, 0)
+    lax.fori_loop(0, cblocks, coarse_relaxed, 0, unroll=16)
     for r in range(0, 24, 8):
         tcoarse[cblocks, r : r + 8, :] = zero
 
@@ -304,7 +319,7 @@
             return nxt, rn, turned, value
 
         u = tcoarse[0, 8:16, :]
-        carry = lax.fori_loop(0, cblocks, body, (u, pltpu.roll(u, L - 1, 1), zero, zero))
+        carry = lax.fori_loop(0, cblocks, body, (u, pltpu.roll(u, L - 1, 1), zero, zero), unroll=16)
         dwin[cblocks, :, :] = jnp.where(lane < L // 2, carry[3], 0.0)
 
     for k in range(groups):
@@ -319,14 +334,6 @@
             send(t < last_t, remote(piece, rd.at[t, :, 8:16, :], d_send.at[k, 1], d_recv.at[t, 1], (c, s)))
         send((t < last_t - 1) & has_down, remote(piece, rd.at[t, :, 0:8, :], d_send.at[k, 0], d_recv.at[t, 0], (c, s + 1)))
         send((t < last_t - 1) & has_up, remote(piece, rd.at[t, :, 16:24, :], d_send.at[k, 2], d_recv.at[t, 2], (c, s - 1)))
-
-    @pl.when(has_up)
-    def _():
-        remote(wsrc, win.at[:, :, 8:16, :], w_send.at[0], w_recv.at[0], (t, s)).wait_recv()
-
-    @pl.when(has_down)
-    def _():
-        remote(wsrc, win.at[:, :, 24:32, :], w_send.at[1], w_recv.at[1], (t, s)).wait_recv()
 
     row = lax.broadcasted_iota(jnp.int32, (8, L), 0)
     keep = {}
@@ -413,10 +420,7 @@
                     out[8 * p : 8 * p + 8, f * L : (f + 1) * L] = tall + u0[f, TOP + 8 * p : TOP + 8 * p + 8, :]
     store = pltpu.make_async_copy(out, out_hbm.at[0], out_sem)
     store.start()
-    for cond, copy in sends:
-        @pl.when(cond)
-        def _(copy=copy):
-            copy.wait_send()
+    drain()
     store.wait()
 
 
@@ -447,7 +451,7 @@
                 dma(groups, 3), dma(groups, 3), dma(groups), dma(groups),
             ],
             compiler_params=pltpu.CompilerParams(
-                collective_id=0, has_side_effects=True, vmem_limit_bytes=40 * 2**20
+                collective_id=0, has_side_effects=True, vmem_limit_bytes=60 * 2**20
             ),
         )(guesses, cond_x, cond_y, source, inflow)
 

time: 51 us -> 34.8 us (0.68)
  Pallas kernels: 45.4 us -> 33 us
  local copies, waits for them, and re-layouts: 5.34 us -> 1.67 us
    pallas_call x1, Pallas kernels: 45.4 us -> 33 us  [shards(): pl.pallas_call(functools.partial(kernel, groups, strips), out_shape=jax.S...]
    unnamed x11 -> x1, local copies, waits for them, and re-layouts: 5.34 us -> 1.67 us
where the time goes in v2:
time: 34.8 us; the launch traced here: 34.6 us
  Pallas kernels  33 us (95%)
  local copies, waits for them, and re-layouts  1.67 us (5%)
    pallas_call x1, Pallas kernels, shards(): pl.pallas_call(functools.partial(kernel, groups, strips), out_shape=jax.S...  33 us
    unnamed x1, local copies, waits for them, and re-layouts  1.67 us

profile of v2, /device:TPU:135, one launch (start us, length us, event | category | flops | bytes accessed | tf_op | source)
XLA Modules:
  0.0 34.6 jit_solution(5533449667550218632)
XLA Ops:
  0.0 33.0 %shard_map.55 = f32[1,16,4096]{2,1,0:T(8,128)} custom-call(f32[1,16,4096]{2,1,0:T(8,128)} %guess_in.1, f32[16,4096]{1,0:T(8,128)} %cx_in.1, f32[16,4096]{1,0:T(8,128)} %cy_in.1, f32[16,4096]{1,0:T(8,128)} %source_in.1, f32[8,2048]{1,0:T(8,128)} %inflow_in.1), custom_call_target="tpu_custom_call" | custom-call | tf_op jit(solution)/shard_map/pallas_call | solution.py:437
  33.0 1.7 %copy.7 = f32[1,16,4096]{2,1,0:T(8,128)} copy(f32[1,16,4096]{2,1,0:T(8,128)} %shard_map.55) | data formatting | bytes 524288

commit v3 on v2

--- a/solution.py
+++ b/solution.py
@@ -10,6 +10,7 @@
 MESH = pl.DeviceIdType.MESH
 F32 = jnp.float32
 L = 128
+ENDS = (10, 20, 28)
 TOP = 16
 
 
@@ -46,16 +47,25 @@
     return total + flow - west, turned
 
 
-def fine_step(src, dst, cx, cy, source, first, tiles, last_strip, blocks, unroll=32):
+def fine_step(src, dst, co, first, tiles, last_strip, start, stop):
+    cx, cy, source = (co.at[i] for i in range(3))
     lane = lane_index()
     row = lax.broadcasted_iota(jnp.int32, (8, L), 0)
     rows = [first + 8 * k for k in range(tiles)]
     outside = [None if r + 8 <= TOP + 16 else (row + r >= TOP + 16) & last_strip for r in rows]
-
-    def body(b, carry):
-        new = []
+    state = []
+    for r in rows:
+        u = src[start, r : r + 8, :]
+        ru = pltpu.roll(u, L - 1, 1)
+        turned = jnp.zeros((8, L), F32)
+        if start > 0:
+            west = src[start - 1, r : r + 8, :]
+            right = jnp.where(lane == L - 1, ru, pltpu.roll(west, L - 1, 1))
+            turned = pltpu.roll(cy[start - 1, r : r + 8, :] * (right - west), 1, 1)
+        state.append((u, ru, turned))
+    for b in range(start, stop):
         for k, r in enumerate(rows):
-            u, ru, turned = carry[k]
+            u, ru, turned = state[k]
             nxt = src[b + 1, r : r + 8, :]
             rn = pltpu.roll(nxt, L - 1, 1)
             right = jnp.where(lane == L - 1, rn, ru)
@@ -67,20 +77,13 @@
             if outside[k] is not None:
                 out = jnp.where(outside[k], 0.0, out)
             dst[b, r : r + 8, :] = out
-            new.append((nxt, rn, turned))
-        return tuple(new)
-
-    start = []
-    for r in rows:
-        u = src[0, r : r + 8, :]
-        start.append((u, pltpu.roll(u, L - 1, 1), jnp.zeros((8, L), F32)))
-    lax.fori_loop(0, blocks, body, tuple(start), unroll=unroll)
+            state[k] = (nxt, rn, turned)
 
 
 def kernel(
     groups, strips, guess_in, cx_in, cy_in, source_in, inflow_in, out_hbm,
-    stage, flow_stage, own, u0, u1, u2, cx, cy, source, rcx, rcy, inflow, tcoarse, dwin,
-    wsrc, win, fa, fb, rd, fsend, frecv, out,
+    stage, flow_stage, own, u0, u1, u2, co, rcx, rcy, inflow, tcoarse, dwin,
+    last_d, wsrc, win, fa, fb, rd, fsend, frecv, out,
     in_sems, out_sem, a_send, a_recv, w_send, w_recv, d_send, d_recv, f_send, f_recv,
 ):
     t = lax.axis_index("tm")
@@ -130,16 +133,16 @@
     for b in range(blocks):
         cols = slice(b * L, (b + 1) * L)
         own[b, :, :] = stage[0, :, cols]
-        cx[b, TOP : TOP + 16, :] = stage[1, :, cols]
-        cy[b, TOP : TOP + 16, :] = stage[2, :, cols]
-        source[b, TOP : TOP + 16, :] = stage[3, :, cols]
+        for i in range(3):
+            co[i, b, TOP : TOP + 16, :] = stage[1 + i, :, cols]
     pl.semaphore_wait(barrier, groups * near - 1)
 
     up_rows, down_rows, main_rows = slice(TOP - 8, TOP), slice(TOP + 16, TOP + 24), slice(TOP, TOP + 16)
     ahead = lax.rem(t + 1, groups)
     mate = jnp.where(even, t + 1, t - 1)
-    coefs = (cx, cy, source)
     inner = u0.at[0:blocks]
+    ends = [e for e in ENDS if e < blocks] + [blocks]
+    chunks = [slice(a, e) for a, e in zip([0] + ends[:-1], ends)]
 
     def send(cond, copy):
         sends.append((cond, copy))
@@ -148,15 +151,25 @@
         def _():
             copy.start()
 
-    for i, ref in enumerate(coefs):
-        send(even & has_down, remote(ref.at[:, TOP + 8 : TOP + 16, :], ref.at[:, up_rows, :], a_send.at[i], a_recv.at[i], (t, s + 1)))
-        send(~even & has_up, remote(ref.at[:, TOP : TOP + 8, :], ref.at[:, down_rows, :], a_send.at[3 + i], a_recv.at[3 + i], (t, s - 1)))
-    guess_down, guess_up = own.at[:, 8:16, :], own.at[:, 0:8, :]
-    send((t < last_t) & has_down, remote(guess_down, inner.at[:, up_rows, :], a_send.at[6], a_recv.at[6], (ahead, s + 1)))
-    send((t < last_t) & has_up, remote(guess_up, inner.at[:, down_rows, :], a_send.at[7], a_recv.at[7], (ahead, s - 1)))
-    send(t < last_t, remote(own, inner.at[:, main_rows, :], a_send.at[8], a_recv.at[8], (ahead, s)))
-    send((t == 0) & has_down, remote(guess_down, inner.at[:, up_rows, :], a_send.at[9], a_recv.at[6], (t, s + 1)))
-    send((t == 0) & has_up, remote(guess_up, inner.at[:, down_rows, :], a_send.at[10], a_recv.at[7], (t, s - 1)))
+    def coef_copy(q, up, sender, where, handed=False):
+        rows = up_rows if up else down_rows
+        edge = slice(TOP + 8, TOP + 16) if up else slice(TOP, TOP + 8)
+        there = co.at[:, chunks[q], rows, :]
+        return remote(there if handed else co.at[:, chunks[q], edge, :], there, a_send.at[sender, q], a_recv.at[0 if up else 1, q], where)
+
+    def guess_copy(q, kind, sender, where):
+        rows = (slice(8, 16), slice(0, 8), slice(0, 16))[kind]
+        there = (up_rows, down_rows, main_rows)[kind]
+        return remote(own.at[chunks[q], rows, :], inner.at[chunks[q], there, :], a_send.at[sender, q], a_recv.at[2 + kind, q], where)
+
+    for q in range(len(chunks)):
+        send(even & has_down, coef_copy(q, True, 0, (t, s + 1)))
+        send(~even & has_up, coef_copy(q, False, 0, (t, s - 1)))
+        send((t < last_t) & has_down, guess_copy(q, 0, 2, (ahead, s + 1)))
+        send((t < last_t) & has_up, guess_copy(q, 1, 3, (ahead, s - 1)))
+        send(t < last_t, guess_copy(q, 2, 4, (ahead, s)))
+        send((t == 0) & has_down, guess_copy(q, 0, 5, (t, s + 1)))
+        send((t == 0) & has_up, guess_copy(q, 1, 6, (t, s - 1)))
 
     for ref in (rcx, rcy, inflow):
         rows = ref.shape[1]
@@ -167,8 +180,8 @@
         inflow[b + 1, :, :] = flow_stage[:, b * L : (b + 1) * L]
 
     def coarse_coefs(b, c):
-        rcx[b + 1, 8:16, :] = restrict_block(cx, b, TOP, lane)
-        rcy[b + 1, 8:16, :] = restrict_block(cy, b, TOP, lane)
+        rcx[b + 1, 8:16, :] = restrict_block(co.at[0], b, TOP, lane)
+        rcy[b + 1, 8:16, :] = restrict_block(co.at[1], b, TOP, lane)
         return c
 
     lax.fori_loop(0, cblocks, coarse_coefs, 0, unroll=16)
@@ -197,8 +210,8 @@
 
     @pl.when(~has_up)
     def _():
-        for ref in (cx, cy, source):
-            clear(ref, up_rows)
+        for i in range(3):
+            clear(co.at[i], up_rows)
         clear(inner, up_rows)
         for i in range(3):
             for a in range(3):
@@ -208,8 +221,8 @@
 
     @pl.when(~has_down)
     def _():
-        for ref in (cx, cy, source):
-            clear(ref, down_rows)
+        for i in range(3):
+            clear(co.at[i], down_rows)
         clear(inner, down_rows)
         for i in range(3):
             for a in range(3):
@@ -222,90 +235,78 @@
         for b in range(blocks):
             u0[b, main_rows, :] = own[b, :, :]
 
-    for i, ref in enumerate(coefs):
-        upper, lower = ref.at[:, up_rows, :], ref.at[:, down_rows, :]
-        up_copy = remote(upper, upper, a_send.at[11 + i], a_recv.at[i], (mate, s))
-        down_copy = remote(lower, lower, a_send.at[14 + i], a_recv.at[3 + i], (mate, s))
+    def hand_on(q):
+        up_copy = coef_copy(q, True, 1, (mate, s), handed=True)
+        down_copy = coef_copy(q, False, 1, (mate, s), handed=True)
 
         @pl.when(even & has_up)
-        def _(up_copy=up_copy):
+        def _():
             up_copy.wait_recv()
 
         send(even & has_up, up_copy)
 
         @pl.when(~even & has_down)
-        def _(down_copy=down_copy):
+        def _():
             down_copy.wait_recv()
 
         send(~even & has_down, down_copy)
 
+    def arrive(q):
         @pl.when(~even & has_up)
-        def _(up_copy=up_copy):
-            up_copy.wait_recv()
+        def _():
+            coef_copy(q, True, 1, (mate, s), handed=True).wait_recv()
 
         @pl.when(even & has_down)
-        def _(down_copy=down_copy):
-            down_copy.wait_recv()
-
-    @pl.when(has_up)
-    def _():
-        remote(guess_down, inner.at[:, up_rows, :], a_send.at[6], a_recv.at[6], (t, s)).wait_recv()
-
-    @pl.when(has_down)
-    def _():
-        remote(guess_up, inner.at[:, down_rows, :], a_send.at[7], a_recv.at[7], (t, s)).wait_recv()
-
-    @pl.when(t > 0)
-    def _():
-        remote(own, inner.at[:, main_rows, :], a_send.at[8], a_recv.at[8], (t, s)).wait_recv()
-
-    @pl.when(has_up)
-    def _():
-        remote(wsrc, win.at[:, :, 8:16, :], w_send.at[0], w_recv.at[0], (t, s)).wait_recv()
-
-    @pl.when(has_down)
-    def _():
-        remote(wsrc, win.at[:, :, 24:32, :], w_send.at[1], w_recv.at[1], (t, s)).wait_recv()
-
-    step = functools.partial(fine_step, cx=cx, cy=cy, source=source, last_strip=~has_down, blocks=blocks)
-
-    @pl.when(t > 0)
-    def _():
-        def pair(i, c):
-            step(u0, u1, first=TOP - 8, tiles=4)
-            step(u1, u0, first=TOP - 8, tiles=4)
-            return c
-
-        lax.fori_loop(0, 2, pair, 0)
-
-    def coarse_relaxed(b, c):
-        rcx[b + 1, 0:8, :] = restrict_block(cx, b, 0, lane)
-        for k in range(3):
-            value = restrict_block(u0, b, 16 * k, lane)
-            tcoarse[b, 8 * k : 8 * k + 8, :] = jnp.where(t > 0, value, 0.0)
-        return c
-
-    lax.fori_loop(0, cblocks, coarse_relaxed, 0, unroll=16)
-    for r in range(0, 24, 8):
-        tcoarse[cblocks, r : r + 8, :] = zero
-
-    @pl.when(~has_down)
-    def _():
-        def body(b, c):
-            tcoarse[b, 16:24, :] = zero
-            return c
-
-        lax.fori_loop(0, cblocks, body, 0)
-
-    @pl.when(t < last_t)
-    def _():
-        step(u0, u1, first=TOP - 4, tiles=3)
-        step(u1, u2, first=TOP - 4, tiles=3)
-        step(u2, u1, first=TOP - 4, tiles=3)
-        step(u1, u2, first=TOP, tiles=2)
-
-        def body(b, carry):
-            u, ru, turned, before = carry
+        def _():
+            coef_copy(q, False, 1, (mate, s), handed=True).wait_recv()
+
+        @pl.when(has_up)
+        def _():
+            guess_copy(q, 0, 2, (t, s)).wait_recv()
+
+        @pl.when(has_down)
+        def _():
+            guess_copy(q, 1, 3, (t, s)).wait_recv()
+
+        @pl.when(t > 0)
+        def _():
+            guess_copy(q, 2, 4, (t, s)).wait_recv()
+
+    plan = [
+        (u0, u1, -8, 4), (u1, u0, -8, 4), (u0, u1, -8, 4), (u1, u0, -4, 3),
+        (u0, u1, -4, 3), (u1, u2, -4, 3), (u2, u1, -4, 3), (u1, u2, 0, 2),
+    ]
+
+    def ready(end, lag):
+        return blocks if end == blocks else max(0, end - lag)
+
+    def steps(levels, before, end):
+        for level in levels:
+            src, dst, first, tiles = plan[level - 1]
+            start, stop = ready(before, level) if before else 0, ready(end, level)
+            if start < stop:
+                fine_step(src, dst, co, TOP + first, tiles, ~has_down, start, stop)
+
+    def coarse_relaxed(start, stop):
+        for b in range(start, stop):
+            rcx[b + 1, 0:8, :] = restrict_block(co.at[0], b, 0, lane)
+            for k in range(3):
+                value = restrict_block(u0, b, 16 * k, lane)
+                drop = t == 0
+                if k == 2:
+                    drop = drop | ~has_down
+                tcoarse[b, 8 * k : 8 * k + 8, :] = jnp.where(drop, 0.0, value)
+
+    def differences(start, stop):
+        u = tcoarse[start, 8:16, :]
+        ru = pltpu.roll(u, L - 1, 1)
+        turned = before = zero
+        if start > 0:
+            west = tcoarse[start - 1, 8:16, :]
+            right = jnp.where(lane == L - 1, ru, pltpu.roll(west, L - 1, 1))
+            turned = pltpu.roll(rcy[start, 8:16, :] * (right - west), 1, 1)
+            before = last_d[...]
+        for b in range(start, stop):
             nxt = tcoarse[b + 1, 8:16, :]
             rn = pltpu.roll(nxt, L - 1, 1)
             right = jnp.where(lane == L - 1, rn, ru)
@@ -316,24 +317,73 @@
             value = restrict_block(u2, b, TOP, lane) - (u + change)
             value = pltpu.roll(value, L // 2, 1)
             dwin[b, :, :] = jnp.where(lane < L // 2, before, value)
-            return nxt, rn, turned, value
-
-        u = tcoarse[0, 8:16, :]
-        carry = lax.fori_loop(0, cblocks, body, (u, pltpu.roll(u, L - 1, 1), zero, zero), unroll=16)
-        dwin[cblocks, :, :] = jnp.where(lane < L // 2, carry[3], 0.0)
-
-    for k in range(groups):
-        c = lax.rem(t + k, groups)
-        piece = dwin.at[pl.ds(2 * c, 3)]
-        if k == 0:
-            @pl.when(t < last_t)
+            u, ru, before = nxt, rn, value
+        last_d[...] = before
+        if stop == cblocks:
+            dwin[cblocks, :, :] = jnp.where(lane < L // 2, before, 0.0)
+
+    def halo_rows(j):
+        return 2 * ((last_t - j) // 2)
+
+    def window_copy(c, j, part, where):
+        halo = halo_rows(j)
+        mine = (slice(8 - halo, 8), slice(0, 8), slice(0, halo))[part]
+        there = (slice(8 - halo, 8), slice(8, 16), slice(16, 16 + halo))[part]
+        return remote(
+            dwin.at[pl.ds(2 * c, 3), mine, :], rd.at[t if where else j, :, there, :],
+            d_send.at[c, part], d_recv.at[t if where else j, part], where or (t, s),
+        )
+
+    def windows(start, stop):
+        for k in range(stop - start):
+            c = start + lax.rem(t + k, stop - start)
+
+            @pl.when((c == t) & (t < last_t))
             def _():
                 for i in range(3):
                     rd[t, i, 8:16, :] = dwin[2 * t + i, :, :]
-        else:
-            send(t < last_t, remote(piece, rd.at[t, :, 8:16, :], d_send.at[k, 1], d_recv.at[t, 1], (c, s)))
-        send((t < last_t - 1) & has_down, remote(piece, rd.at[t, :, 0:8, :], d_send.at[k, 0], d_recv.at[t, 0], (c, s + 1)))
-        send((t < last_t - 1) & has_up, remote(piece, rd.at[t, :, 16:24, :], d_send.at[k, 2], d_recv.at[t, 2], (c, s - 1)))
+
+            send((c != t) & (t < last_t), window_copy(c, 0, 1, (c, s)))
+            for j in range(0, last_t - 1, 2):
+                among = (t >= j) & (t < j + 2)
+                send(among & has_down, window_copy(c, j + 1, 0, (c, s + 1)))
+                send(among & has_up, window_copy(c, j + 1, 2, (c, s - 1)))
+
+    for r in range(0, 24, 8):
+        tcoarse[cblocks, r : r + 8, :] = zero
+    hand_on(0)
+    end = t_done = d_done = w_done = 0
+    for q in range(len(chunks)):
+        if q + 1 < len(chunks):
+            hand_on(q + 1)
+        arrive(q)
+        before, end = end, ends[q]
+        t_from, t_done = t_done, ready(end, 4) // 2
+        d_from, d_done = d_done, ready(end, 8) // 2
+        w_from, w_done = w_done, groups if end == blocks else max(0, (d_done - 1) // 2)
+
+        @pl.when(t > 0)
+        def _():
+            steps((1, 2, 3, 4), before, end)
+
+        coarse_relaxed(t_from, t_done)
+
+        @pl.when(t < last_t)
+        def _():
+            steps((5, 6, 7, 8), before, end)
+            if d_from < d_done:
+                differences(d_from, d_done)
+
+        if w_from < w_done:
+            windows(w_from, w_done)
+
+    @pl.when(has_up)
+    def _():
+        remote(wsrc, win.at[:, :, 8:16, :], w_send.at[0], w_recv.at[0], (t, s)).wait_recv()
+
+    @pl.when(has_down)
+    def _():
+        remote(wsrc, win.at[:, :, 24:32, :], w_send.at[1], w_recv.at[1], (t, s)).wait_recv()
 
     row = lax.broadcasted_iota(jnp.int32, (8, L), 0)
     keep = {}
@@ -352,20 +402,19 @@
     now, later = fa, fb
     for g in range(1, groups):
         j = g - 1
-        piece = dwin.at[pl.ds(0, 3)]
 
         @pl.when(t != j)
         def _():
-            remote(piece, rd.at[j, :, 8:16, :], d_send.at[0, 1], d_recv.at[j, 1], (t, s)).wait_recv()
+            window_copy(0, j, 1, None).wait_recv()
 
         if j < last_t - 1:
             @pl.when(has_up)
             def _():
-                remote(piece, rd.at[j, :, 0:8, :], d_send.at[0, 0], d_recv.at[j, 0], (t, s)).wait_recv()
+                window_copy(0, j, 0, None).wait_recv()
 
             @pl.when(has_down)
             def _():
-                remote(piece, rd.at[j, :, 16:24, :], d_send.at[0, 2], d_recv.at[j, 2], (t, s)).wait_recv()
+                window_copy(0, j, 2, None).wait_recv()
 
         middle = []
         for k in range(3):
@@ -442,12 +491,12 @@
             scratch_shapes=[
                 vmem(4, rows, columns), vmem(rows // 2, columns // 2), vmem(blocks, rows, L),
                 vmem(blocks + 1, 48, L), vmem(blocks + 1, 48, L), vmem(blocks + 1, 48, L),
-                vmem(blocks, 48, L), vmem(blocks, 48, L), vmem(blocks, 48, L),
+                vmem(3, blocks, 48, L),
                 vmem(cblocks + 2, 24, L), vmem(cblocks + 2, 24, L), vmem(cblocks + 2, 8, L),
                 vmem(cblocks + 1, 24, L), vmem(cblocks + 1, 8, L),
-                vmem(3, 3, 8, L), vmem(3, 3, 40, L), vmem(3, 40, L), vmem(3, 40, L),
+                vmem(8, L), vmem(3, 3, 8, L), vmem(3, 3, 40, L), vmem(3, 40, L), vmem(3, 40, L),
                 vmem(groups - 1, 3, 24, L), vmem(groups, 2, 8, L), vmem(cblocks, 8, L), vmem(rows, columns),
-                dma(5), pltpu.SemaphoreType.DMA, dma(17), dma(9), dma(2), dma(2),
+                dma(5), pltpu.SemaphoreType.DMA, dma(7, 8), dma(5, 8), dma(2), dma(2),
                 dma(groups, 3), dma(groups, 3), dma(groups), dma(groups),
             ],
             compiler_params=pltpu.CompilerParams(

time: 34.8 us -> 34.7 us (level)
  Pallas kernels: 33 us -> 32.6 us
    pallas_call x1, Pallas kernels: 33 us -> 32.6 us  [shards(): pl.pallas_call(functools.partial(kernel, groups, strips), out_shape=jax.S...]
where the time goes in v3:
time: 34.7 us; the launch traced here: 34.2 us
  Pallas kernels  32.6 us (94%)
  local copies, waits for them, and re-layouts  1.67 us (5%)
    pallas_call x1, Pallas kernels, shards(): pl.pallas_call(functools.partial(kernel, groups, strips), out_shape=jax.S...  32.6 us
    unnamed x1, local copies, waits for them, and re-layouts  1.67 us

profile of v3, /device:TPU:135, one launch (start us, length us, event | category | flops | bytes accessed | tf_op | source)
XLA Modules:
  0.0 34.2 jit_solution(15589516096686332848)
XLA Ops:
  0.0 32.6 %shard_map.55 = f32[1,16,4096]{2,1,0:T(8,128)} custom-call(f32[1,16,4096]{2,1,0:T(8,128)} %guess_in.1, f32[16,4096]{1,0:T(8,128)} %cx_in.1, f32[16,4096]{1,0:T(8,128)} %cy_in.1, f32[16,4096]{1,0:T(8,128)} %source_in.1, f32[8,2048]{1,0:T(8,128)} %inflow_in.1), custom_call_target="tpu_custom_call" | custom-call | tf_op jit(solution)/shard_map/pallas_call | solution.py:486
  32.6 1.7 %copy.7 = f32[1,16,4096]{2,1,0:T(8,128)} copy(f32[1,16,4096]{2,1,0:T(8,128)} %shard_map.55) | data formatting | bytes 524288

commit v4 on v0

v4 whole, which is shorter than its diff:
```python
import functools

import jax
import jax.numpy as jnp
from jax import lax
from jax.experimental import pallas as pl
from jax.experimental.pallas import tpu as pltpu
from jax.sharding import PartitionSpec as P

MESH = pl.DeviceIdType.MESH
F32 = jnp.float32
L = 128
H = L // 2
TOP = 16
UP, DOWN, MAIN = slice(TOP - 8, TOP), slice(TOP + 16, TOP + 24), slice(TOP, TOP + 16)
PAIRS = ((0, 1), (7, 6), (2, 3), (5, 4))


def remote(src, dst, send, recv, where):
    return pltpu.make_async_remote_copy(
        src_ref=src, dst_ref=dst, send_sem=send, recv_sem=recv, device_id=where, device_id_type=MESH
    )


def gather(value, index, axis):
    return jnp.take_along_axis(value, index, axis=axis, mode="promise_in_bounds")


def restrict_block(ref, block, row, lane):
    halves = []
    for q in range(2):
        if 2 * block + q >= ref.shape[0]:
            halves.append(jnp.zeros((8, L), F32))
            continue
        pair = ref[2 * block + q, pl.ds(row, 8, stride=2), :] + ref[
            2 * block + q, pl.ds(row + 1, 8, stride=2), :
        ]
        pair = pair + pltpu.roll(pair, L - 1, 1)
        halves.append(gather(pair, (2 * lane) % L, 1))
    return jnp.where(lane < H, halves[0], halves[1]) * 0.25


def fluxes(u, right, up, down, cx, cx_up, cy, carry, lane):
    flow = cy * (right - u)
    turned = pltpu.roll(flow, 1, 1)
    west = jnp.where(lane == 0, carry, turned)
    total = cx * (down - u) - cx_up * (u - up)
    return total + flow - west, turned


def fine_step(pairs, co, first, tiles, last_strip, last_window):
    cx, cy, source = (co.at[i] for i in range(3))
    blocks = co.shape[1]
    lane = lax.broadcasted_iota(jnp.int32, (8, L), 1)
    row = lax.broadcasted_iota(jnp.int32, (8, L), 0)
    zero = jnp.zeros((8, L), F32)
    rows = [first + 8 * k for k in range(tiles)]
    below = [None if r + 8 <= TOP + 16 else (row + r >= TOP + 16) & last_strip for r in rows]
    beyond = (lane >= H) & last_window
    state = {}
    for n, (src, _) in enumerate(pairs):
        for k, r in enumerate(rows):
            u = src[0, r : r + 8, :]
            state[n, k] = (u, pltpu.roll(u, L - 1, 1), zero)
    for b in range(blocks):
        for n, (src, dst) in enumerate(pairs):
            for k, r in enumerate(rows):
                u, ru, turned = state[n, k]
                nxt, rn = zero, zero
                if b + 1 < blocks:
                    nxt = src[b + 1, r : r + 8, :]
                    rn = pltpu.roll(nxt, L - 1, 1)
                right = jnp.where(lane == L - 1, rn, ru)
                change, turned = fluxes(
                    u, right, src[b, r - 1 : r + 7, :], src[b, r + 1 : r + 9, :],
                    cx[b, r : r + 8, :], cx[b, r - 1 : r + 7, :], cy[b, r : r + 8, :], turned, lane,
                )
                out = u + change + source[b, r : r + 8, :]
                drop = below[k]
                if b + 1 == blocks:
                    drop = beyond if drop is None else drop | beyond
                if drop is not None:
                    out = jnp.where(drop, 0.0, out)
                dst[b, r : r + 8, :] = out
                state[n, k] = (nxt, rn, turned)


def kernel(
    groups, strips, guess_in, cx_in, cy_in, source_in, inflow_in, out_hbm,
    stage, flow_stage, shifted, guess, relaxed, ua, ub, co, tcoarse, wsrc, win, rd, fa, fb, outw,
    in_sems, g_send, g_recv, c_send, c_recv, w_send, w_recv, d_send, d_recv, o_send, o_recv, own_sem,
):
    t = lax.axis_index("tm")
    s = lax.axis_index("space")
    has_up, has_down = s > 0, s < strips - 1
    last = groups - 1
    lane = lax.broadcasted_iota(jnp.int32, (8, L), 1)
    row = lax.broadcasted_iota(jnp.int32, (8, L), 0)
    zero = jnp.zeros((8, L), F32)
    blocks = shifted.shape[0] - 1
    width = blocks // groups
    cwidth = width // 2
    wb = width + 1
    sends = []

    def send(cond, copy):
        sends.append((cond, copy))

        @pl.when(cond)
        def _():
            copy.start()

    def drain():
        for cond, copy in sends:
            @pl.when(cond)
            def _(copy=copy):
                copy.wait_send()

    loads = [
        pltpu.make_async_copy(ref, stage.at[i], in_sems.at[i])
        for i, ref in enumerate((guess_in.at[0], cx_in, cy_in, source_in))
    ]
    loads.append(pltpu.make_async_copy(inflow_in, flow_stage, in_sems.at[4]))
    for load in loads:
        load.start()

    barrier = pltpu.get_barrier_semaphore()
    for k in range(1, groups):
        pl.semaphore_signal(barrier, inc=1, device_id=(lax.rem(t + k, groups), s), device_id_type=MESH)

    @pl.when(has_up)
    def _():
        for k in range(groups):
            pl.semaphore_signal(barrier, inc=1, device_id=(lax.rem(t + k, groups), s - 1), device_id_type=MESH)

    @pl.when(has_down)
    def _():
        for k in range(groups):
            pl.semaphore_signal(barrier, inc=1, device_id=(lax.rem(t + k, groups), s + 1), device_id_type=MESH)

    near = 3 - jnp.where(has_up, 0, 1) - jnp.where(has_down, 0, 1)

    for load in loads:
        load.wait()
    for r in range(0, 16, 8):
        before = zero
        for b in range(blocks):
            turned = pltpu.roll(stage[0, r : r + 8, b * L : (b + 1) * L], H, 1)
            shifted[b, r : r + 8, :] = jnp.where(lane < H, before, turned)
            before = turned
        shifted[blocks, r : r + 8, :] = jnp.where(lane < H, before, 0.0)

    def around(ref, a, rows, count, per):
        values = []
        for n in range(-1, count + 1):
            at = jnp.clip(t * per + n, 0, per * groups - 1)
            cols = pl.ds(pl.multiple_of(at * L, L), L)
            value = ref[rows, cols] if a is None else ref[a, rows, cols]
            if n < 0:
                value = jnp.where(t == 0, 0.0, value)
            if n == count:
                value = jnp.where(t == last, 0.0, value)
            values.append(value)
        return values

    for a in range(3):
        for r in range(0, 16, 8):
            turned = [pltpu.roll(v, H, 1) for v in around(stage, 1 + a, slice(r, r + 8), width, width)]
            for i in range(wb):
                co[a, i, TOP + r : TOP + r + 8, :] = jnp.where(lane < H, turned[i], turned[i + 1])
    pl.semaphore_wait(barrier, groups * near - 1)

    def guess_copy(k, part, where):
        c = lax.rem(t - k + groups, groups)
        mine = (slice(0, 16), slice(8, 16), slice(0, 8))[part]
        there = (MAIN, UP, DOWN)[part]
        return remote(
            shifted.at[pl.ds(width * c, wb), mine, :], guess.at[k, :, there, :],
            g_send.at[part, k], g_recv.at[part, k], where or (c, s + (0, 1, -1)[part]),
        )

    send(has_down, remote(co.at[:, :, TOP + 8 : TOP + 16, :], co.at[:, :, UP, :], c_send.at[0], c_recv.at[0], (t, s + 1)))
    send(has_up, remote(co.at[:, :, TOP : TOP + 8, :], co.at[:, :, DOWN, :], c_send.at[1], c_recv.at[1], (t, s - 1)))
    for k in [k for pair in PAIRS for k in pair]:
        send((t < last) & has_down, guess_copy(k, 1, None))
        send((t < last) & has_up, guess_copy(k, 2, None))
        if k > 0:
            send(t < last, guess_copy(k, 0, None))

    turned = [pltpu.roll(v, H // 2, 1) for v in around(flow_stage, None, slice(0, 8), cwidth, cwidth)]
    for i in range(cwidth + 1):
        value = jnp.where(lane < H // 2, turned[i], turned[i + 1])
        for a in range(3):
            if a > 0:
                value = restrict_block(co.at[a - 1], i, TOP, lane)
            wsrc[a, i, :, :] = value
            win[a, i, 16:24, :] = value
    w_down = remote(wsrc, win.at[:, :, 8:16, :], w_send.at[0], w_recv.at[0], (t, s + 1))
    w_up = remote(wsrc, win.at[:, :, 24:32, :], w_send.at[1], w_recv.at[1], (t, s - 1))
    send(has_down, w_down)
    send(has_up, w_up)

    def clear(fine, coarse, halo):
        for i in range(wb):
            for a in range(3):
                co[a, i, fine, :] = zero
            for k in range(groups):
                guess[k, i, fine, :] = zero
        for i in range(cwidth + 1):
            for a in range(3):
                win[a, i, coarse, :] = zero
            for j in range(groups):
                rd[j, i, halo, :] = zero

    @pl.when(~has_up)
    def _():
        clear(UP, slice(8, 16), slice(0, 8))

    @pl.when(~has_down)
    def _():
        clear(DOWN, slice(24, 32), slice(16, 24))

    for i in range(wb):
        guess[0, i, MAIN, :] = shifted[width * t + i, :, :]

    @pl.when(has_up)
    def _():
        remote(co.at[:, :, TOP + 8 : TOP + 16, :], co.at[:, :, UP, :], c_send.at[0], c_recv.at[0], (t, s)).wait_recv()
        remote(wsrc, win.at[:, :, 8:16, :], w_send.at[0], w_recv.at[0], (t, s)).wait_recv()

    @pl.when(has_down)
    def _():
        remote(co.at[:, :, TOP : TOP + 8, :], co.at[:, :, DOWN, :], c_send.at[1], c_recv.at[1], (t, s)).wait_recv()
        remote(wsrc, win.at[:, :, 24:32, :], w_send.at[1], w_recv.at[1], (t, s)).wait_recv()

    def arrive(k):
        held = lax.rem(t + k, groups) < last

        @pl.when(held & has_up)
        def _():
            guess_copy(k, 1, (t, s)).wait_recv()

        @pl.when(held & has_down)
        def _():
            guess_copy(k, 2, (t, s)).wait_recv()

        if k > 0:
            @pl.when(held)
            def _():
                guess_copy(k, 0, (t, s)).wait_recv()

    step = functools.partial(fine_step, co=co, last_strip=~has_down, last_window=t == last)
    for pair in PAIRS:
        for k in pair:
            arrive(k)
        g0, r0 = [guess.at[k] for k in pair], [relaxed.at[k] for k in pair]
        a0, b0 = [ua.at[n] for n in range(2)], [ub.at[n] for n in range(2)]
        for src, dst, first, tiles in (
            (g0, a0, -8, 4), (a0, b0, -8, 4), (b0, a0, -8, 4), (a0, r0, -4, 3),
            (r0, a0, -4, 3), (a0, b0, -4, 3), (b0, a0, -4, 3), (a0, b0, 0, 2),
        ):
            step(list(zip(src, dst)), first=TOP + first, tiles=tiles)
        for n, k in enumerate(pair):
            o = lax.rem(t + k, groups) + 1
            for i in range(cwidth + 1):
                for m in range(3):
                    value = restrict_block(relaxed.at[k], i, 16 * m, lane)
                    if m == 2:
                        value = jnp.where(has_down, value, 0.0)
                    tcoarse[o, i, 8 * m : 8 * m + 8, :] = value
        for n, k in enumerate(pair):
            o = lax.rem(t + k, groups) + 1
            turned = zero
            for i in range(cwidth + 1):
                u = tcoarse[o, i, 8:16, :]
                rn = pltpu.roll(tcoarse[o, i + 1, 8:16, :], L - 1, 1) if i < cwidth else zero
                right = jnp.where(lane == L - 1, rn, pltpu.roll(u, L - 1, 1))
                change, turned = fluxes(
                    u, right, tcoarse[o, i, 7:15, :], tcoarse[o, i, 9:17, :],
                    win[1, i, 16:24, :], win[1, i, 15:23, :], win[2, i, 16:24, :], turned, lane,
                )
                rd[o, i, 8:16, :] = restrict_block(ub.at[n], i, TOP, lane) - (u + change)
    for i in range(cwidth + 1):
        rd[0, i, 8:16, :] = tcoarse[1, i, 8:16, :]

    def d_copy(j, part, where):
        halo = last - 1 - j
        mine = (slice(16 - halo, 16), slice(8, 8 + halo))[part]
        there = (slice(8 - halo, 8), slice(16, 16 + halo))[part]
        both = slice(j, j + 2)
        return remote(rd.at[both, :, mine, :], rd.at[both, :, there, :], d_send.at[part, j], d_recv.at[part, j], where)

    for j in range(0, last - 1, 2):
        send(has_down, d_copy(j, 0, (t, s + 1)))
        send(has_up, d_copy(j, 1, (t, s - 1)))

    for g in range(groups):
        k = lax.rem(g - 1 - t + 2 * groups, groups) if g > 0 else lax.rem(groups - t, groups)
        ref = relaxed if g > 0 else guess
        for r in range(0, 16, 8):
            turned = [pltpu.roll(ref[k, i, TOP + r : TOP + r + 8, :], H, 1) for i in range(wb)]
            for i in range(width):
                outw[g, r : r + 8, i * L : (i + 1) * L] = jnp.where(lane < H, turned[i], turned[i + 1])

    def finish(g, error):
        for i in range(width):
            base = H // 2 + H * i
            at = base % L + lane // 2
            wide = gather(error[base // L], at % L, 1)
            if base % L + H > L:
                wide = jnp.where(at < L, wide, gather(error[base // L + 1], at % L, 1))
            for p in range(2):
                tall = gather(wide, row // 2 + 4 * p, 0)
                rows, cols = slice(8 * p, 8 * p + 8), slice(i * L, (i + 1) * L)
                outw[g, rows, cols] = outw[g, rows, cols] + tall
        send(t != g, out_copy(g, t, (g, s)))

        @pl.when(t == g)
        def _():
            own_copy(g).start()

    def out_copy(g, c, where):
        cols = pl.ds(pl.multiple_of(c * (width * L), L), width * L)
        return remote(outw.at[g], out_hbm.at[0, :, cols], o_send.at[g], o_recv.at[c], where)

    def own_copy(g):
        cols = pl.ds(pl.multiple_of(t * (width * L), L), width * L)
        return pltpu.make_async_copy(outw.at[g], out_hbm.at[0, :, cols], own_sem)

    finish(0, [win[0, i, 16:24, :] for i in range(cwidth + 1)])

    keep = {}
    for k in range(3):
        for i in range(cwidth + 1):
            bad = jnp.broadcast_to(~has_down, (8, L)) if k == 2 else None
            if i == cwidth:
                beyond = (lane >= H // 2) & (t == last)
                bad = beyond if bad is None else bad | beyond
            keep[k, i] = bad
    now, later = win.at[0], fa
    for g in range(1, groups):
        j = g - 1
        if j % 2 == 0 and j < last - 1:
            @pl.when(has_up)
            def _():
                d_copy(j, 0, (t, s)).wait_recv()

            @pl.when(has_down)
            def _():
                d_copy(j, 1, (t, s)).wait_recv()

        error = []
        for k in range(3):
            if g == last and k != 1:
                continue
            r = 8 + 8 * k
            turned = zero
            for i in range(cwidth + 1):
                u = now[i, r : r + 8, :]
                rn = pltpu.roll(now[i + 1, r : r + 8, :], L - 1, 1) if i < cwidth else zero
                right = jnp.where(lane == L - 1, rn, pltpu.roll(u, L - 1, 1))
                change, turned = fluxes(
                    u, right, now[i, r - 1 : r + 7, :], now[i, r + 1 : r + 9, :],
                    win[1, i, r : r + 8, :], win[1, i, r - 1 : r + 7, :], win[2, i, r : r + 8, :], turned, lane,
                )
                value = u + change + rd[j, i, 8 * k : 8 * k + 8, :]
                if keep[k, i] is not None:
                    value = jnp.where(keep[k, i], 0.0, value)
                if g < last:
                    later[i, r : r + 8, :] = value
                if k == 1:
                    error.append(value - tcoarse[g, i, 8:16, :])
        now, later = later, (fb if later is fa else fa)
        finish(g, error)

    for c in range(groups):
        @pl.when(t != c)
        def _():
            out_copy(0, c, (t, s)).wait_recv()

    drain()
    own_copy(0).wait()


def solution(mesh):
    groups, strips = mesh.shape["tm"], mesh.shape["space"]

    def shards(guesses, cond_x, cond_y, source, inflow):
        _, rows, columns = guesses.shape
        blocks = columns // L
        assert rows == 16 and groups == 8 and blocks == 4 * groups
        vmem = lambda *shape: pltpu.VMEM(shape, F32)
        dma = lambda *shape: pltpu.SemaphoreType.DMA(shape)
        return pl.pallas_call(
            functools.partial(kernel, groups, strips),
            out_shape=jax.ShapeDtypeStruct(guesses.shape, F32),
            in_specs=[pl.BlockSpec(memory_space=pl.ANY)] * 5,
            out_specs=pl.BlockSpec(memory_space=pl.ANY),
            scratch_shapes=[
                vmem(4, rows, columns), vmem(rows // 2, columns // 2), vmem(blocks + 1, rows, L),
                vmem(groups, 5, 48, L), vmem(groups, 5, 48, L), vmem(2, 5, 48, L), vmem(2, 5, 48, L),
                vmem(3, 5, 48, L), vmem(groups + 1, 3, 24, L), vmem(3, 3, 8, L), vmem(3, 3, 40, L),
                vmem(groups + 1, 3, 24, L), vmem(3, 40, L), vmem(3, 40, L), vmem(groups, rows, 4 * L),
                dma(5), dma(3, groups), dma(3, groups), dma(2), dma(2), dma(2), dma(2),
                dma(2, groups), dma(2, groups), dma(groups), dma(groups), pltpu.SemaphoreType.DMA,
            ],
            compiler_params=pltpu.CompilerParams(
                collective_id=0, has_side_effects=True, vmem_limit_bytes=60 * 2**20
            ),
        )(guesses, cond_x, cond_y, source, inflow)

    return jax.shard_map(
        shards,
        mesh=mesh,
        in_specs=(
            P("tm", "space", None),
            P("space", None),
            P("space", None),
            P("space", None),
            P("space", None),
        ),
        out_specs=P("tm", "space", None),
        check_vma=False,
    )
```

time: 337 us -> 33.4 us (0.10)
  the two profiles are of different devices: /device:TPU:122 before, /device:TPU:135 now
where the time goes in v4:
time: 33.4 us; the launch traced here: 33.1 us
  Pallas kernels  31.4 us (94%)
  local copies, waits for them, and re-layouts  1.67 us (5%)
    pallas_call x1, Pallas kernels, shards(): pl.pallas_call(functools.partial(kernel, groups, strips), out_shape=jax.S...  31.4 us
    unnamed x1, local copies, waits for them, and re-layouts  1.67 us

profile of v4, /device:TPU:135, one launch (start us, length us, event | category | flops | bytes accessed | tf_op | source)
XLA Modules:
  0.0 33.1 jit_solution(5825527822125153324)
XLA Ops:
  0.0 31.4 %shard_map.55 = f32[1,16,4096]{2,1,0:T(8,128)} custom-call(f32[1,16,4096]{2,1,0:T(8,128)} %guess_in.1, f32[16,4096]{1,0:T(8,128)} %cx_in.1, f32[16,4096]{1,0:T(8,128)} %cy_in.1, f32[16,4096]{1,0:T(8,128)} %source_in.1, f32[8,2048]{1,0:T(8,128)} %inflow_in.1), custom_call_target="tpu_custom_call" | custom-call | tf_op jit(solution)/shard_map/pallas_call | solution.py:394
  31.4 1.7 %copy.7 = f32[1,16,4096]{2,1,0:T(8,128)} copy(f32[1,16,4096]{2,1,0:T(8,128)} %shard_map.55) | data formatting | bytes 524288

commit v5 on v4

--- a/solution.py
+++ b/solution.py
@@ -13,7 +13,9 @@
 H = L // 2
 TOP = 16
 UP, DOWN, MAIN = slice(TOP - 8, TOP), slice(TOP + 16, TOP + 24), slice(TOP, TOP + 16)
-PAIRS = ((0, 1), (7, 6), (2, 3), (5, 4))
+ROUNDS = ((0, 1, 7, 2), (3, 4, 5, 6))
+SPLIT = False
+BATCHES = (2, 4, 6, 7)
 
 
 def remote(src, dst, send, recv, where):
@@ -115,6 +117,7 @@
             @pl.when(cond)
             def _(copy=copy):
                 copy.wait_send()
+        sends.clear()
 
     loads = [
         pltpu.make_async_copy(ref, stage.at[i], in_sems.at[i])
@@ -181,11 +184,16 @@
 
     send(has_down, remote(co.at[:, :, TOP + 8 : TOP + 16, :], co.at[:, :, UP, :], c_send.at[0], c_recv.at[0], (t, s + 1)))
     send(has_up, remote(co.at[:, :, TOP : TOP + 8, :], co.at[:, :, DOWN, :], c_send.at[1], c_recv.at[1], (t, s - 1)))
-    for k in [k for pair in PAIRS for k in pair]:
-        send((t < last) & has_down, guess_copy(k, 1, None))
-        send((t < last) & has_up, guess_copy(k, 2, None))
-        if k > 0:
-            send(t < last, guess_copy(k, 0, None))
+    def send_guesses(slots):
+        for k in slots:
+            send((t < last) & has_down, guess_copy(k, 1, None))
+            send((t < last) & has_up, guess_copy(k, 2, None))
+            if k > 0:
+                send(t < last, guess_copy(k, 0, None))
+
+    send_guesses(ROUNDS[0])
+    if not SPLIT:
+        send_guesses(ROUNDS[1])
 
     turned = [pltpu.roll(v, H // 2, 1) for v in around(flow_stage, None, slice(0, 8), cwidth, cwidth)]
     for i in range(cwidth + 1):
@@ -223,6 +231,10 @@
     for i in range(wb):
         guess[0, i, MAIN, :] = shifted[width * t + i, :, :]
 
+    if SPLIT:
+        drain()
+        send_guesses(ROUNDS[1])
+
     @pl.when(has_up)
     def _():
         remote(co.at[:, :, TOP + 8 : TOP + 16, :], co.at[:, :, UP, :], c_send.at[0], c_recv.at[0], (t, s)).wait_recv()
@@ -250,11 +262,11 @@
                 guess_copy(k, 0, (t, s)).wait_recv()
 
     step = functools.partial(fine_step, co=co, last_strip=~has_down, last_window=t == last)
-    for pair in PAIRS:
+    for pair in ROUNDS:
         for k in pair:
             arrive(k)
         g0, r0 = [guess.at[k] for k in pair], [relaxed.at[k] for k in pair]
-        a0, b0 = [ua.at[n] for n in range(2)], [ub.at[n] for n in range(2)]
+        a0, b0 = [ua.at[n] for n in range(len(pair))], [ub.at[n] for n in range(len(pair))]
         for src, dst, first, tiles in (
             (g0, a0, -8, 4), (a0, b0, -8, 4), (b0, a0, -8, 4), (a0, r0, -4, 3),
             (r0, a0, -4, 3), (a0, b0, -4, 3), (b0, a0, -4, 3), (a0, b0, 0, 2),
@@ -263,11 +275,9 @@
         for n, k in enumerate(pair):
             o = lax.rem(t + k, groups) + 1
             for i in range(cwidth + 1):
-                for m in range(3):
-                    value = restrict_block(relaxed.at[k], i, 16 * m, lane)
-                    if m == 2:
-                        value = jnp.where(has_down, value, 0.0)
-                    tcoarse[o, i, 8 * m : 8 * m + 8, :] = value
+                tcoarse[o, i, 7:15, :] = restrict_block(relaxed.at[k], i, TOP - 2, lane)
+                value = restrict_block(relaxed.at[k], i, TOP + 2, lane)
+                tcoarse[o, i, 9:17, :] = jnp.where((row == 7) & ~has_down, 0.0, value)
         for n, k in enumerate(pair):
             o = lax.rem(t + k, groups) + 1
             turned = zero
@@ -313,11 +323,14 @@
                 tall = gather(wide, row // 2 + 4 * p, 0)
                 rows, cols = slice(8 * p, 8 * p + 8), slice(i * L, (i + 1) * L)
                 outw[g, rows, cols] = outw[g, rows, cols] + tall
-        send(t != g, out_copy(g, t, (g, s)))
-
-        @pl.when(t == g)
-        def _():
-            own_copy(g).start()
+
+    def send_windows(start, stop):
+        for g in range(start, stop):
+            send(t != g, out_copy(g, t, (g, s)))
+
+            @pl.when(t == g)
+            def _():
+                own_copy(g).start()
 
     def out_copy(g, c, where):
         cols = pl.ds(pl.multiple_of(c * (width * L), L), width * L)
@@ -328,6 +341,7 @@
         return pltpu.make_async_copy(outw.at[g], out_hbm.at[0, :, cols], own_sem)
 
     finish(0, [win[0, i, 16:24, :] for i in range(cwidth + 1)])
+    send_windows(0, 1)
 
     keep = {}
     for k in range(3):
@@ -337,18 +351,18 @@
                 beyond = (lane >= H // 2) & (t == last)
                 bad = beyond if bad is None else bad | beyond
             keep[k, i] = bad
+    for j in range(0, last - 1, 2):
+        @pl.when(has_up)
+        def _():
+            d_copy(j, 0, (t, s)).wait_recv()
+
+        @pl.when(has_down)
+        def _():
+            d_copy(j, 1, (t, s)).wait_recv()
+
     now, later = win.at[0], fa
     for g in range(1, groups):
         j = g - 1
-        if j % 2 == 0 and j < last - 1:
-            @pl.when(has_up)
-            def _():
-                d_copy(j, 0, (t, s)).wait_recv()
-
-            @pl.when(has_down)
-            def _():
-                d_copy(j, 1, (t, s)).wait_recv()
-
         error = []
         for k in range(3):
             if g == last and k != 1:
@@ -372,6 +386,8 @@
                     error.append(value - tcoarse[g, i, 8:16, :])
         now, later = later, (fb if later is fa else fa)
         finish(g, error)
+        if g in BATCHES:
+            send_windows(max([1] + [b + 1 for b in BATCHES if b < g]), g + 1)
 
     for c in range(groups):
         @pl.when(t != c)
@@ -398,7 +414,7 @@
             out_specs=pl.BlockSpec(memory_space=pl.ANY),
             scratch_shapes=[
                 vmem(4, rows, columns), vmem(rows // 2, columns // 2), vmem(blocks + 1, rows, L),
-                vmem(groups, 5, 48, L), vmem(groups, 5, 48, L), vmem(2, 5, 48, L), vmem(2, 5, 48, L),
+                vmem(groups, 5, 48, L), vmem(groups, 5, 48, L), vmem(4, 5, 48, L), vmem(4, 5, 48, L),
                 vmem(3, 5, 48, L), vmem(groups + 1, 3, 24, L), vmem(3, 3, 8, L), vmem(3, 3, 40, L),
                 vmem(groups + 1, 3, 24, L), vmem(3, 40, L), vmem(3, 40, L), vmem(groups, rows, 4 * L),
                 dma(5), dma(3, groups), dma(3, groups), dma(2), dma(2), dma(2), dma(2),

time: 33.4 us -> 31.4 us (0.940)
  Pallas kernels: 31.4 us -> 29.4 us
    pallas_call x1, Pallas kernels: 31.4 us -> 29.4 us  [shards(): pl.pallas_call(functools.partial(kernel, groups, strips), out_shape=jax.S...]
where the time goes in v5:
time: 31.4 us; the launch traced here: 31.1 us
  Pallas kernels  29.4 us (94%)
  local copies, waits for them, and re-layouts  1.67 us (5%)
    pallas_call x1, Pallas kernels, shards(): pl.pallas_call(functools.partial(kernel, groups, strips), out_shape=jax.S...  29.4 us
    unnamed x1, local copies, waits for them, and re-layouts  1.67 us

profile of v5, /device:TPU:135, one launch (start us, length us, event | category | flops | bytes accessed | tf_op | source)
XLA Modules:
  0.0 31.1 jit_solution(6998028101764806729)
XLA Ops:
  0.0 29.4 %shard_map.55 = f32[1,16,4096]{2,1,0:T(8,128)} custom-call(f32[1,16,4096]{2,1,0:T(8,128)} %guess_in.1, f32[16,4096]{1,0:T(8,128)} %cx_in.1, f32[16,4096]{1,0:T(8,128)} %cy_in.1, f32[16,4096]{1,0:T(8,128)} %source_in.1, f32[8,2048]{1,0:T(8,128)} %inflow_in.1), custom_call_target="tpu_custom_call" | custom-call | tf_op jit(solution)/shard_map/pallas_call | solution.py:410
  29.4 1.7 %copy.7 = f32[1,16,4096]{2,1,0:T(8,128)} copy(f32[1,16,4096]{2,1,0:T(8,128)} %shard_map.55) | data formatting | bytes 524288

commit v6 on v5

--- a/solution.py
+++ b/solution.py
@@ -13,8 +13,8 @@
 H = L // 2
 TOP = 16
 UP, DOWN, MAIN = slice(TOP - 8, TOP), slice(TOP + 16, TOP + 24), slice(TOP, TOP + 16)
-ROUNDS = ((0, 1, 7, 2), (3, 4, 5, 6))
-SPLIT = False
+ORDER = (4, 3, 5, 2, 6, 1, 7, 0)
+ROUNDS = ((0, 1, 2, 3, 4, 5, 6),)
 BATCHES = (2, 4, 6, 7)
 
 
@@ -143,8 +143,7 @@
 
     near = 3 - jnp.where(has_up, 0, 1) - jnp.where(has_down, 0, 1)
 
-    for load in loads:
-        load.wait()
+    loads[0].wait()
     for r in range(0, 16, 8):
         before = zero
         for b in range(blocks):
@@ -166,34 +165,32 @@
             values.append(value)
         return values
 
+    pl.semaphore_wait(barrier, groups * near - 1)
+
+    def guess_copy(g, k, part, where):
+        c = lax.rem(t + k, groups)
+        mine = (slice(0, 16), slice(8, 16), slice(0, 8))[part]
+        there = (MAIN, UP, DOWN)[part]
+        return remote(
+            shifted.at[pl.ds(width * c, wb), mine, :], guess.at[g, :, there, :],
+            g_send.at[part, k], g_recv.at[part, g], where or (c, s + (0, 1, -1)[part]),
+        )
+
+    for k in ORDER:
+        send((t < last) & has_down, guess_copy(t, k, 1, None))
+        send((t < last) & has_up, guess_copy(t, k, 2, None))
+        if k > 0:
+            send(t < last, guess_copy(t, k, 0, None))
+
+    for load in loads[1:]:
+        load.wait()
     for a in range(3):
         for r in range(0, 16, 8):
             turned = [pltpu.roll(v, H, 1) for v in around(stage, 1 + a, slice(r, r + 8), width, width)]
             for i in range(wb):
                 co[a, i, TOP + r : TOP + r + 8, :] = jnp.where(lane < H, turned[i], turned[i + 1])
-    pl.semaphore_wait(barrier, groups * near - 1)
-
-    def guess_copy(k, part, where):
-        c = lax.rem(t - k + groups, groups)
-        mine = (slice(0, 16), slice(8, 16), slice(0, 8))[part]
-        there = (MAIN, UP, DOWN)[part]
-        return remote(
-            shifted.at[pl.ds(width * c, wb), mine, :], guess.at[k, :, there, :],
-            g_send.at[part, k], g_recv.at[part, k], where or (c, s + (0, 1, -1)[part]),
-        )
-
     send(has_down, remote(co.at[:, :, TOP + 8 : TOP + 16, :], co.at[:, :, UP, :], c_send.at[0], c_recv.at[0], (t, s + 1)))
     send(has_up, remote(co.at[:, :, TOP : TOP + 8, :], co.at[:, :, DOWN, :], c_send.at[1], c_recv.at[1], (t, s - 1)))
-    def send_guesses(slots):
-        for k in slots:
-            send((t < last) & has_down, guess_copy(k, 1, None))
-            send((t < last) & has_up, guess_copy(k, 2, None))
-            if k > 0:
-                send(t < last, guess_copy(k, 0, None))
-
-    send_guesses(ROUNDS[0])
-    if not SPLIT:
-        send_guesses(ROUNDS[1])
 
     turned = [pltpu.roll(v, H // 2, 1) for v in around(flow_stage, None, slice(0, 8), cwidth, cwidth)]
     for i in range(cwidth + 1):
@@ -212,8 +209,8 @@
         for i in range(wb):
             for a in range(3):
                 co[a, i, fine, :] = zero
-            for k in range(groups):
-                guess[k, i, fine, :] = zero
+            for g in range(last):
+                guess[g, i, fine, :] = zero
         for i in range(cwidth + 1):
             for a in range(3):
                 win[a, i, coarse, :] = zero
@@ -228,12 +225,10 @@
     def _():
         clear(DOWN, slice(24, 32), slice(16, 24))
 
-    for i in range(wb):
-        guess[0, i, MAIN, :] = shifted[width * t + i, :, :]
-
-    if SPLIT:
-        drain()
-        send_guesses(ROUNDS[1])
+    @pl.when(t < last)
+    def _():
+        for i in range(wb):
+            guess[t, i, MAIN, :] = shifted[width * t + i, :, :]
 
     @pl.when(has_up)
     def _():
@@ -245,49 +240,53 @@
         remote(co.at[:, :, TOP : TOP + 8, :], co.at[:, :, DOWN, :], c_send.at[1], c_recv.at[1], (t, s)).wait_recv()
         remote(wsrc, win.at[:, :, 24:32, :], w_send.at[1], w_recv.at[1], (t, s)).wait_recv()
 
-    def arrive(k):
-        held = lax.rem(t + k, groups) < last
-
-        @pl.when(held & has_up)
-        def _():
-            guess_copy(k, 1, (t, s)).wait_recv()
-
-        @pl.when(held & has_down)
-        def _():
-            guess_copy(k, 2, (t, s)).wait_recv()
-
-        if k > 0:
-            @pl.when(held)
-            def _():
-                guess_copy(k, 0, (t, s)).wait_recv()
+    def arrive(g):
+        @pl.when(has_up)
+        def _():
+            guess_copy(g, 0, 1, (t, s)).wait_recv()
+
+        @pl.when(has_down)
+        def _():
+            guess_copy(g, 0, 2, (t, s)).wait_recv()
+
+        @pl.when(t != g)
+        def _():
+            guess_copy(g, 0, 0, (t, s)).wait_recv()
 
     step = functools.partial(fine_step, co=co, last_strip=~has_down, last_window=t == last)
-    for pair in ROUNDS:
-        for k in pair:
+    for part in ROUNDS:
+        for k in part:
             arrive(k)
-        g0, r0 = [guess.at[k] for k in pair], [relaxed.at[k] for k in pair]
-        a0, b0 = [ua.at[n] for n in range(len(pair))], [ub.at[n] for n in range(len(pair))]
+        g0, r0 = [guess.at[k] for k in part], [relaxed.at[k] for k in part]
+        a0, b0 = [ua.at[n] for n in range(len(part))], [ub.at[n] for n in range(len(part))]
+        first_pass_done = False
         for src, dst, first, tiles in (
             (g0, a0, -8, 4), (a0, b0, -8, 4), (b0, a0, -8, 4), (a0, r0, -4, 3),
             (r0, a0, -4, 3), (a0, b0, -4, 3), (b0, a0, -4, 3), (a0, b0, 0, 2),
         ):
-            step(list(zip(src, dst)), first=TOP + first, tiles=tiles)
-        for n, k in enumerate(pair):
-            o = lax.rem(t + k, groups) + 1
-            for i in range(cwidth + 1):
+            both = list(zip(src, dst))
+            if src is r0 or first_pass_done:
+                first_pass_done = True
+                both = [pair for k, pair in zip(part, both) if k < last - 1]
+            step(both, first=TOP + first, tiles=tiles)
+        for i in range(cwidth + 1):
+            for n, k in enumerate(part):
+                o = k + 1
                 tcoarse[o, i, 7:15, :] = restrict_block(relaxed.at[k], i, TOP - 2, lane)
                 value = restrict_block(relaxed.at[k], i, TOP + 2, lane)
                 tcoarse[o, i, 9:17, :] = jnp.where((row == 7) & ~has_down, 0.0, value)
-        for n, k in enumerate(pair):
-            o = lax.rem(t + k, groups) + 1
-            turned = zero
-            for i in range(cwidth + 1):
+        turned = {k: zero for k in part}
+        for i in range(cwidth + 1):
+            for n, k in enumerate(part):
+                o = k + 1
+                if o == last:
+                    continue
                 u = tcoarse[o, i, 8:16, :]
                 rn = pltpu.roll(tcoarse[o, i + 1, 8:16, :], L - 1, 1) if i < cwidth else zero
                 right = jnp.where(lane == L - 1, rn, pltpu.roll(u, L - 1, 1))
-                change, turned = fluxes(
+                change, turned[k] = fluxes(
                     u, right, tcoarse[o, i, 7:15, :], tcoarse[o, i, 9:17, :],
-                    win[1, i, 16:24, :], win[1, i, 15:23, :], win[2, i, 16:24, :], turned, lane,
+                    win[1, i, 16:24, :], win[1, i, 15:23, :], win[2, i, 16:24, :], turned[k], lane,
                 )
                 rd[o, i, 8:16, :] = restrict_block(ub.at[n], i, TOP, lane) - (u + change)
     for i in range(cwidth + 1):
@@ -305,7 +304,7 @@
         send(has_up, d_copy(j, 1, (t, s - 1)))
 
     for g in range(groups):
-        k = lax.rem(g - 1 - t + 2 * groups, groups) if g > 0 else lax.rem(groups - t, groups)
+        k = max(g - 1, 0)
         ref = relaxed if g > 0 else guess
         for r in range(0, 16, 8):
             turned = [pltpu.roll(ref[k, i, TOP + r : TOP + r + 8, :], H, 1) for i in range(wb)]
@@ -414,9 +413,9 @@
             out_specs=pl.BlockSpec(memory_space=pl.ANY),
             scratch_shapes=[
                 vmem(4, rows, columns), vmem(rows // 2, columns // 2), vmem(blocks + 1, rows, L),
-                vmem(groups, 5, 48, L), vmem(groups, 5, 48, L), vmem(4, 5, 48, L), vmem(4, 5, 48, L),
-                vmem(3, 5, 48, L), vmem(groups + 1, 3, 24, L), vmem(3, 3, 8, L), vmem(3, 3, 40, L),
-                vmem(groups + 1, 3, 24, L), vmem(3, 40, L), vmem(3, 40, L), vmem(groups, rows, 4 * L),
+                vmem(groups - 1, 5, 48, L), vmem(groups - 1, 5, 48, L), vmem(groups - 1, 5, 48, L), vmem(groups - 1, 5, 48, L),
+                vmem(3, 5, 48, L), vmem(groups, 3, 24, L), vmem(3, 3, 8, L), vmem(3, 3, 40, L),
+                vmem(groups, 3, 24, L), vmem(3, 40, L), vmem(3, 40, L), vmem(groups, rows, 4 * L),
                 dma(5), dma(3, groups), dma(3, groups), dma(2), dma(2), dma(2), dma(2),
                 dma(2, groups), dma(2, groups), dma(groups), dma(groups), pltpu.SemaphoreType.DMA,
             ],

time: 31.4 us -> 30.6 us (0.975)
  Pallas kernels: 29.4 us -> 28.6 us
    pallas_call x1, Pallas kernels: 29.4 us -> 28.6 us  [shards(): pl.pallas_call(functools.partial(kernel, groups, strips), out_shape=jax.S...]
where the time goes in v6:
time: 30.6 us; the launch traced here: 30.3 us
  Pallas kernels  28.6 us (93%)
  local copies, waits for them, and re-layouts  1.67 us (5%)
    pallas_call x1, Pallas kernels, shards(): pl.pallas_call(functools.partial(kernel, groups, strips), out_shape=jax.S...  28.6 us
    unnamed x1, local copies, waits for them, and re-layouts  1.67 us

profile of v6, /device:TPU:135, one launch (start us, length us, event | category | flops | bytes accessed | tf_op | source)
XLA Modules:
  0.0 30.3 jit_solution(15022906098979454333)
XLA Ops:
  0.0 28.6 %shard_map.55 = f32[1,16,4096]{2,1,0:T(8,128)} custom-call(f32[1,16,4096]{2,1,0:T(8,128)} %guess_in.1, f32[16,4096]{1,0:T(8,128)} %cx_in.1, f32[16,4096]{1,0:T(8,128)} %cy_in.1, f32[16,4096]{1,0:T(8,128)} %source_in.1, f32[8,2048]{1,0:T(8,128)} %inflow_in.1), custom_call_target="tpu_custom_call" | custom-call | tf_op jit(solution)/shard_map/pallas_call | solution.py:409
  28.6 1.7 %copy.7 = f32[1,16,4096]{2,1,0:T(8,128)} copy(f32[1,16,4096]{2,1,0:T(8,128)} %shard_map.55) | data formatting | bytes 524288

commit v7 on v6

--- a/solution.py
+++ b/solution.py
@@ -420,9 +420,9 @@
                 dma(2, groups), dma(2, groups), dma(groups), dma(groups), pltpu.SemaphoreType.DMA,
             ],
             compiler_params=pltpu.CompilerParams(
-                collective_id=0, has_side_effects=True, vmem_limit_bytes=60 * 2**20
+                collective_id=0, has_side_effects=True, vmem_limit_bytes=40 * 2**20
             ),
-        )(guesses, cond_x, cond_y, source, inflow)
+        )(*(pltpu.with_memory_space_constraint(x, pltpu.MemorySpace.HBM) for x in (guesses, cond_x, cond_y, source, inflow)))
 
     return jax.shard_map(
         shards,

time: 30.6 us -> 29.5 us (0.964)
  local copies, waits for them, and re-layouts: 1.67 us -> 0.71 us
    unnamed x1, local copies, waits for them, and re-layouts: 1.67 us -> 0.71 us
where the time goes in v7:
time: 29.5 us; the launch traced here: 29.3 us
  Pallas kernels  28.5 us (97%)
  local copies, waits for them, and re-layouts  0.71 us (2%)
    pallas_call x1, Pallas kernels, shards(): pl.pallas_call(functools.partial(kernel, groups, strips), out_shape=jax.S...  28.5 us
    unnamed x1, local copies, waits for them, and re-layouts  0.71 us

profile of v7, /device:TPU:135, one launch (start us, length us, event | category | flops | bytes accessed | tf_op | source)
XLA Modules:
  0.0 29.3 jit_solution(197913900737376930)
XLA Ops:
  0.0 28.5 %shard_map.55 = f32[1,16,4096]{2,1,0:T(8,128)S(1)} custom-call(f32[1,16,4096]{2,1,0:T(8,128)} %guess_in.1, f32[16,4096]{1,0:T(8,128)} %cx_in.1, f32[16,4096]{1,0:T(8,128)} %cy_in.1, f32[16,4096]{1,0:T(8,128)} %source_in.1, f32[8,2048]{1,0:T(8,128)} %inflow_in.1), custom_call_target="tpu_custom_call" | custom-call | tf_op jit(solution)/shard_map/pallas_call | solution.py:409
  28.5 0.7 %copy.7 = f32[1,16,4096]{2,1,0:T(8,128)} copy(f32[1,16,4096]{2,1,0:T(8,128)S(1)} %shard_map.55) | data formatting | bytes 524288

commit v8 on v7

--- a/solution.py
+++ b/solution.py
@@ -124,8 +124,7 @@
         for i, ref in enumerate((guess_in.at[0], cx_in, cy_in, source_in))
     ]
     loads.append(pltpu.make_async_copy(inflow_in, flow_stage, in_sems.at[4]))
-    for load in loads:
-        load.start()
+    loads[0].start()
 
     barrier = pltpu.get_barrier_semaphore()
     for k in range(1, groups):
@@ -144,6 +143,8 @@
     near = 3 - jnp.where(has_up, 0, 1) - jnp.where(has_down, 0, 1)
 
     loads[0].wait()
+    for load in loads[1:]:
+        load.start()
     for r in range(0, 16, 8):
         before = zero
         for b in range(blocks):

time: 29.5 us -> 29.5 us (level)
  no operation moved by 1% of the time
where the time goes in v8:
time: 29.5 us; the launch traced here: 29.2 us
  Pallas kernels  28.5 us (97%)
  local copies, waits for them, and re-layouts  0.71 us (2%)
    pallas_call x1, Pallas kernels, shards(): pl.pallas_call(functools.partial(kernel, groups, strips), out_shape=jax.S...  28.5 us
    unnamed x1, local copies, waits for them, and re-layouts  0.71 us

profile of v8, /device:TPU:135, one launch (start us, length us, event | category | flops | bytes accessed | tf_op | source)
XLA Modules:
  0.0 29.2 jit_solution(12162825048574089645)
XLA Ops:
  0.0 28.5 %shard_map.55 = f32[1,16,4096]{2,1,0:T(8,128)S(1)} custom-call(f32[1,16,4096]{2,1,0:T(8,128)} %guess_in.1, f32[16,4096]{1,0:T(8,128)} %cx_in.1, f32[16,4096]{1,0:T(8,128)} %cy_in.1, f32[16,4096]{1,0:T(8,128)} %source_in.1, f32[8,2048]{1,0:T(8,128)} %inflow_in.1), custom_call_target="tpu_custom_call" | custom-call | tf_op jit(solution)/shard_map/pallas_call | solution.py:410
  28.5 0.7 %copy.7 = f32[1,16,4096]{2,1,0:T(8,128)} copy(f32[1,16,4096]{2,1,0:T(8,128)S(1)} %shard_map.55) | data formatting | bytes 524288
